TPU v7x, 32 devices: a whole 2x2x4 slice. The times are simulated.
32 devices in a mesh: space: 8 (over z, y), mem: 4 (over x, core).
Axes of the slice: x: 2, y: 2, z: 4, core: 2. Of those that a mesh axis runs over, the one named last changes fastest.
Arguments:
- prior_ensemble: float32 [512, 32, 128], P('mem', 'space'), may hold values from -70 to 70
- stencil_factors: float32 [4, 32, 128], P(None, 'space'), may hold values from 0.02 to 0.22
- sea_mask: int32 [32, 128], P('space'), may hold values 0 or 1
- measured_site_positions: int32 [8, 128], P('space'), may hold values from 0 to 511
- measured_data: float32 [1024], P('space'), may hold values from -16 to 16
- measurement_precision: float32 [1024], P('space'), may hold values from 0.5 to 2
- cotangent: float32 [512, 32, 128], P('mem', 'space'), may hold values from -6 to 6
Outputs:
- grad_prior: float32 [512, 32, 128], P('mem', 'space')
- grad_coef: float32 [4, 32, 128], P(None, 'space')
Inputs may be any that keep to these rules, and one draw needn't show every extreme that they name: `measured_site_positions`: the flat position row * 128 + column, within its strip of 4 rows, of each observed cell; strip s holds rows s * 4 to (s + 1) * 4 - 1. `sea_mask`: 1 marks a sea cell, 0 a land cell.
All inputs are finite; a program needn't handle non-finite values. No bound on the sum of `sea_mask` on one device may be relied on, other than what follows from the above.
Results may differ from a plain program's by a relative error of at most 0.0003.
Values sent between devices are 32-bit elements; how exact they have to be, the bound alone decides.
A program may use at most 64 MiB of HBM per device.

v0:
```python
import jax
import jax.numpy as jnp
from jax import lax
from jax.sharding import PartitionSpec as P

SAMPLE_TOTAL = 512


highest = lax.Precision.HIGHEST


def extended_2(block, sides, width):
    for axis, dim in sides:
        count = lax.axis_size(axis)
        forward = [(i, i + 1) for i in range(count - 1)]
        backward = [(target, source) for source, target in forward]
        low = lax.ppermute(
            lax.slice_in_dim(block, block.shape[dim] - width, None, axis=dim), axis, forward
        )
        high = lax.ppermute(lax.slice_in_dim(block, 0, width, axis=dim), axis, backward)
        block = jnp.concatenate([low, block, high], axis=dim)
    return block


def matmul(left_side, right_side):
    return jnp.dot(left_side, right_side, precision=highest, preferred_element_type=jnp.float32)


def contract(left_side, right_side, left_dim, right_dim):
    return lax.dot_general(
        left_side,
        right_side,
        (((left_dim,), (right_dim,)), ((), ())),
        precision=highest,
        preferred_element_type=jnp.float32,
    )


def neighbours(extended):
    center = extended[:, 1:-1]
    northern = extended[:, :-2]
    southern = extended[:, 2:]
    border = jnp.zeros_like(center[..., :1])
    western = jnp.concatenate([border, center[..., :-1]], axis=-1)
    eastern = jnp.concatenate([center[..., 1:], border], axis=-1)
    return (center, northern, southern, western, eastern)


def substep(extended, stencil_factors, ocean_share):
    center, northern, southern, western, eastern = neighbours(extended)
    advanced = (
        center
        + stencil_factors[0] * (northern - center)
        + stencil_factors[1] * (southern - center)
        + stencil_factors[2] * (western - center)
        + stencil_factors[3] * (eastern - center)
    )
    return ocean_share * advanced


def transpose_step(weight_ext, coef_ext):
    center = weight_ext[:, 1:-1]
    inner_coef = coef_ext[:, 1:-1]
    from_south = coef_ext[0, 2:] * weight_ext[:, 2:]
    from_north = coef_ext[1, :-2] * weight_ext[:, :-2]
    spread_west = inner_coef[2] * center
    spread_east = inner_coef[3] * center
    border = jnp.zeros_like(center[..., :1])
    from_east = jnp.concatenate([spread_west[..., 1:], border], axis=-1)
    from_west = jnp.concatenate([border, spread_east[..., :-1]], axis=-1)
    keeping = 1.0 - inner_coef[0] - inner_coef[1] - inner_coef[2] - inner_coef[3]
    return center * keeping + from_south + from_north + from_east + from_west


def coef_terms(weight, extended):
    center, northern, southern, western, eastern = neighbours(extended)
    return jnp.stack(
        [
            jnp.sum(weight * (northern - center), axis=0),
            jnp.sum(weight * (southern - center), axis=0),
            jnp.sum(weight * (western - center), axis=0),
            jnp.sum(weight * (eastern - center), axis=0),
        ]
    )


def single_rims(stacked):
    return extended_2(stacked, (("space", 1),), 1)


def member_total(vector):
    return lax.psum(vector, "mem")


def local(
    prior_ensemble,
    stencil_factors,
    sea_mask,
    measured_site_positions,
    measured_data,
    measurement_precision,
    cotangent,
):
    members, strip_rows, strip_cols = prior_ensemble.shape
    cell_count = strip_rows * strip_cols
    ocean_share = sea_mask.astype(jnp.float32)
    stacked = jnp.concatenate([prior_ensemble, stencil_factors, ocean_share[None]], axis=0)
    narrow = single_rims(stacked)
    prior_ext = narrow[:members]
    coef_ext = narrow[members : members + 4]
    first_state = substep(prior_ext, stencil_factors, ocean_share)
    first_ext = single_rims(first_state)
    second_state = substep(first_ext, stencil_factors, ocean_share)
    onehot = (measured_site_positions[0][:, None] == jnp.arange(cell_count)[None, :]).astype(
        jnp.float32
    )
    state_band_piece = second_state.reshape(members, cell_count)
    picked = contract(state_band_piece, onehot, 1, 1)
    tanh_picked = jnp.tanh(picked)
    observed = picked + 0.5 * tanh_picked
    totals = member_total(
        jnp.concatenate([jnp.sum(state_band_piece, axis=0), jnp.sum(observed, axis=0)])
    )
    sample_average = totals[:cell_count] / SAMPLE_TOTAL
    observed_mean = totals[cell_count:] / SAMPLE_TOTAL
    covariance_factor_matrix = jnp.sqrt(jnp.float32(SAMPLE_TOTAL - 1))
    sample_deviations = (state_band_piece - sample_average) / covariance_factor_matrix
    obs_anom = (observed - observed_mean) * measurement_precision / covariance_factor_matrix
    innovation = measurement_precision * (measured_data - observed_mean)
    cot_rows = cotangent.reshape(members, cell_count)
    cot_full, anom_full = (
        lax.all_gather(cot_rows, "mem", axis=0, tiled=True),
        lax.all_gather(obs_anom, "mem", axis=0, tiled=True),
    )
    offset = lax.axis_index("mem") * members
    gram_rows = contract(obs_anom, anom_full, 1, 1)
    pull_rows = matmul(obs_anom, innovation)
    cross_rows = contract(sample_deviations, cot_full, 1, 1)
    gram_tile, pull_tile, cross_tile = lax.psum((gram_rows, pull_rows, cross_rows), "space")
    gram_sum, obs_pull, cross_sum = (
        lax.all_gather(gram_tile, "mem", axis=0, tiled=True),
        lax.all_gather(pull_tile, "mem", axis=0, tiled=True),
        lax.all_gather(cross_tile, "mem", axis=0, tiled=True),
    )
    identity = jnp.eye(SAMPLE_TOTAL, dtype=jnp.float32)
    system = identity + gram_sum
    norm_scale = jnp.sqrt(jnp.sum(system * system))
    approach = system / norm_scale
    factor_first = 1.5 * identity - 0.5 * approach
    next_rows = matmul(approach, factor_first)
    second_factor = 1.5 * identity - 0.5 * matmul(factor_first, next_rows)
    polar_rows = matmul(second_factor, factor_first)
    transform = polar_rows / jnp.sqrt(norm_scale)
    mid_pull = matmul(transform, obs_pull)
    mean_weights = matmul(transform, mid_pull)
    column_block = lax.dynamic_slice_in_dim(transform, offset, members, 1)
    weight_rows = lax.dynamic_slice_in_dim(mean_weights, offset, members, 0)
    mix_rows = covariance_factor_matrix * column_block.T + weight_rows[:, None]
    anom_bar = matmul(mix_rows, cot_full)
    row_weights = covariance_factor_matrix * jnp.sum(transform, axis=1) + jnp.sum(mean_weights)
    anom_bar_total = matmul(row_weights, cot_full)
    cot_total = jnp.sum(cot_full, axis=0)
    weight_bar = covariance_factor_matrix * cross_sum.T
    mean_bar = jnp.sum(cross_sum, axis=1)
    weight_bar = weight_bar + jnp.outer(mean_bar, mid_pull)
    mid_bar = contract(transform, mean_bar, 0, 0)
    weight_bar = weight_bar + jnp.outer(mid_bar, obs_pull)
    pull_bar = contract(transform, mid_bar, 0, 0)
    scale_bar = -0.5 * jnp.sum(weight_bar * transform) / norm_scale
    polar_bar = weight_bar / jnp.sqrt(norm_scale)
    factor_two_bar = contract(polar_bar, factor_first, 1, 1)
    polar_one_bar = matmul(second_factor, polar_bar)
    product_bar = -0.5 * factor_two_bar
    polar_one_bar = polar_one_bar + contract(product_bar, next_rows, 1, 1)
    next_bar = contract(factor_first, product_bar, 0, 0)
    factor_one_bar = polar_one_bar + contract(approach, next_bar, 0, 0)
    approach_bar = contract(next_bar, factor_first, 1, 1) - 0.5 * factor_one_bar
    system_bar = approach_bar / norm_scale
    scale_bar = scale_bar - jnp.sum(approach_bar * approach) / norm_scale
    system_bar = system_bar + scale_bar * system / norm_scale
    sym_bar = system_bar + system_bar.T
    sym_rows = lax.dynamic_slice_in_dim(sym_bar, offset, members, 0)
    pull_bar_rows = lax.dynamic_slice_in_dim(pull_bar, offset, members, 0)
    obs_anom_bar = matmul(sym_rows, anom_full) + pull_bar_rows[:, None] * innovation[None, :]
    innovation_bar = contract(anom_full, pull_bar, 0, 0)
    obs_anom_total = matmul(jnp.sum(sym_bar, axis=0), anom_full) + jnp.sum(pull_bar) * innovation
    observed_mean_bar = (
        -(obs_anom_total * measurement_precision / covariance_factor_matrix)
        - measurement_precision * innovation_bar
    )
    observed_bar = (
        obs_anom_bar * measurement_precision / covariance_factor_matrix
        + observed_mean_bar / SAMPLE_TOTAL
    )
    picked_bar = observed_bar * (1.0 + 0.5 * (1.0 - tanh_picked * tanh_picked))
    field_bar = (
        anom_bar / covariance_factor_matrix
        + (cot_total - anom_bar_total / covariance_factor_matrix) / SAMPLE_TOTAL
        + matmul(picked_bar, onehot)
    )
    second_bar = ocean_share * field_bar.reshape(members, strip_rows, strip_cols)
    grad_second = coef_terms(second_bar, first_ext)
    bar_ext = single_rims(second_bar)
    first_bar = ocean_share * transpose_step(bar_ext, coef_ext)
    grad_first = coef_terms(first_bar, prior_ext)
    prior_grad = transpose_step(single_rims(first_bar), coef_ext)
    coef_total = member_total((grad_first + grad_second).reshape(-1))
    return (
        prior_grad,
        coef_total.reshape(4, strip_rows, strip_cols) / jnp.sqrt(jnp.float32(SAMPLE_TOTAL)),
    )


def solution(mesh):
    placed = (
        P("mem", "space", None),
        P(None, "space", None),
        P("space", None),
        P("space", None),
        P("space"),
        P("space"),
        P("mem", "space", None),
    )
    return jax.shard_map(
        local,
        mesh=mesh,
        in_specs=placed,
        out_specs=(P("mem", "space", None), P(None, "space", None)),
        check_vma=False,
    )
```

profile of v0, /device:TPU:0, one launch (start us, length us, event | category | flops | bytes accessed | tf_op | source)
XLA Modules:
  0.0 234.4 jit_solution(3785101224762855547)
XLA Ops:
  9.2 4.9 %collective-permute-start = (f32[133,1,128]{2,1,0:T(1,128)S(1)}, f32[133,1,128]{2,1,0:T(1,128)S(1)}, u32[]{:S(2)}, u32[]{:S(2)}) collective-permute-start(f32[133,1,128]{2,1,0:T(1,128)S(1)} %get-tuple-element.23), channel_id=1, source_target_pairs={{0,4},{4,8},{8,12},{12,16},{16,20},{20,24},{24,28},{1,5},{5,9},{9,... | collective-permute-start | bytes 204296 | tf_op jit(solution)/shard_map/ppermute | solution.py:17
  14.1 1.3 collective-permute-start.1
  17.3 3.0 %collective-permute-done.1 = f32[133,1,128]{2,1,0:T(1,128)S(1)} collective-permute-done((f32[133,1,128]{2,1,0:T(1,128)S(1)}, f32[133,1,128]{2,1,0:T(1,128)S(1)}, u32[]{:S(2)}, u32[]{:S(2)}) %collective-permute-start.1) | collective-permute-done | bytes 68128 | tf_op jit(solution)/shard_map/ppermute | solution.py:20
  21.5 4.3 %collective-permute-start.2 = (f32[128,1,128]{2,1,0:T(1,128)S(1)}, f32[128,1,128]{2,1,0:T(1,128)S(1)}, u32[]{:S(2)}, u32[]{:S(2)}) collective-permute-start(f32[128,1,128]{2,1,0:T(1,128)S(1)} %get-tuple-element.35), channel_id=1, source_target_pairs={{0,4},{4,8},{8,12},{12,16},{16,20},{20,24},{24,28},{1,5},{5,9},{9,... | collective-permute-start | bytes 196616 | tf_op jit(solution)/shard_map/ppermute | solution.py:17
  25.8 1.3 collective-permute-start.3
  27.7 4.3 %collective-permute-done.3 = f32[128,1,128]{2,1,0:T(1,128)S(1)} collective-permute-done((f32[128,1,128]{2,1,0:T(1,128)S(1)}, f32[128,1,128]{2,1,0:T(1,128)S(1)}, u32[]{:S(2)}, u32[]{:S(2)}) %collective-permute-start.3) | collective-permute-done | bytes 65568 | tf_op jit(solution)/shard_map/ppermute | solution.py:20
  33.7 5.7 %psum.35 = f32[640]{0:T(1024)S(1)} all-reduce(f32[640]{0:T(1024)S(1)} %pad_maximum_fusion.9), channel_id=1, replica_groups=mesh['space'=8,'mem'=4] {'mem'}, use_global_device_ids=true, to_apply=%region_2.0 | all-reduce | flops 640 | bytes 5120 | tf_op jit(solution)/shard_map/psum | solution.py:92
  39.5 6.0 %all_gather.15 = f32[512,128]{1,0:T(8,128)S(1)} all-gather(f32[128,128]{1,0:T(8,128)S(1)} %multiply_multiply_fusion), channel_id=1, replica_groups=mesh['space'=8,'mem'=4] {'mem'}, dimensions={0}, use_global_device_ids=true | all-gather | bytes 327680 | tf_op jit(solution)/shard_map/all_gather | solution.py:133
  46.5 3.1 %fusion.21 = f32[128,512]{1,0:T(8,128)} fusion(f32[512,512]{1,0:T(8,128)} %all-gather.7.cloned.1.call-done, f32[16,8,4,128]{3,2,1,0:T(4,128)S(1)} %bitcast.128, f32[512]{0:T(512)S(1)} %slice_multiply_fusion.4), kind=kOutput, calls=%fused_computation.45 | convolution fusion | flops 402784256 | bytes 1574912 | tf_op jit(solution)/shard_map/dot_general | solution.py:30
  49.8 73.1 %all-reduce.11.cloned.1.call-done = (f32[128,512]{1,0:T(8,128)}, f32[128,512]{1,0:T(8,128)}) async-done(((f32[128,512]{1,0:T(8,128)}, f32[128,512]{1,0:T(8,128)}), (f32[128,512]{1,0:T(8,128)}, f32[128,512]{1,0:T(8,128)})) %all-reduce.11.cloned.1.call-update) | async-done | bytes 524304 | tf_op jit(solution)/shard_map/psum | solution.py:139
  124.3 19.7 %psum.37 = f32[128]{0:T(128)S(1)} all-reduce(f32[128]{0:T(128)S(1)} %convolution_bitcast_fusion.2), channel_id=1, replica_groups=mesh['space'=8,'mem'=4] {'space'}, use_global_device_ids=true, to_apply=%region_5.0 | all-reduce | flops 128 | bytes 1024 | tf_op jit(solution)/shard_map/psum | solution.py:139
  144.0 5.2 %all-gather = f32[4,1,128]{2,1,0:T(1,128)S(1)} all-gather(f32[1,1,128]{2,1,0:T(1,128)S(1)} %bitcast.163), channel_id=1, replica_groups=mesh['space'=8,'mem'=4] {'mem'}, dimensions={0}, use_global_device_ids=true | all-gather | bytes 2560 | tf_op jit(solution)/shard_map/all_gather | solution.py:142
  149.9 2.2 multiply_reduce_fusion.2
  152.7 2.0 fusion.17
  155.7 2.9 %select_subtract_fusion = f32[512,512]{1,0:T(8,128)} fusion(f32[512,512]{1,0:T(8,128)S(1)} %fusion.17, f32[512,512]{1,0:T(8,128)S(1)} %copy-done.6, f32[]{:T(128)S(6)} %sqrt.7), kind=kOutput, calls=%fused_computation | convolution fusion | flops 1613496320 | bytes 3145732 | tf_op jit(solution)/shard_map/dot_general | solution.py:26
  158.6 1.4 reduce_sum.180
  160.0 3.5 %convolution_divide_fusion = f32[512,512]{0,1:T(8,128)S(1)} fusion(f32[512,512]{1,0:T(8,128)} %select_subtract_fusion, f32[]{:T(128)S(6)} %sqrt.8, f32[512,512]{1,0:T(8,128)} %all-gather.5.cloned.1.call-done, f32[]{:T(128)S(6)} %sqrt.7), kind=kOutput, calls=%fused_computation.7 | convolution fusion | flops 1612709888 | bytes 3145736 | tf_op jit(solution)/shard_map/dot_general | solution.py:26
  170.9 2.5 %multiply_reduce_fusion.1 = (f32[]{:T(128)}, f32[512]{0:T(512)}) fusion(f32[512,512]{0,1:T(8,128)S(1)} %convolution_divide_fusion, f32[512,512]{1,0:T(8,128)} %all-gather.9.cloned.1.call-done, f32[512]{0:T(512)} %bitcast.143, f32[512]{0:T(512)S(1)} %bitcast.138, f32[512]{0:T(512)} %bitcast.140, f32[512]{0:T(512)S(1)} %copy-done.38), kind=kLoop, calls=%fused_computation.32 | loop fusion | flops 2096639 | bytes 2107396 | tf_op jit(solution)/shard_map/reduce_sum | solution.py:169
  174.1 3.4 %fusion.83 = f32[512,512]{1,0:T(8,128)S(1)} fusion(f32[512,512]{1,0:T(8,128)} %select_subtract_fusion, f32[512,512]{1,0:T(8,128)S(1)} %copy-done.8, f32[512]{0:T(512)} %bitcast.144, f32[512]{0:T(512)} %bitcast.137, f32[512]{0:T(512)} %bitcast.141, f32[512]{0:T(512)} %copy-done.37, f32[]{:T(128)S(6)} %sqrt.8), kind=kOutput, calls=%fused_computation.159 | convolution fusion | flops 1612185600 | bytes 3153924 | tf_op jit(solution)/shard_map/dot_general | solution.py:26
  177.6 3.9 %convolution_multiply_fusion = f32[512,512]{1,0:T(8,128)S(1)} fusion(f32[512,512]{1,0:T(8,128)S(1)} %copy-done.8, f32[512]{0:T(512)S(1)} %bitcast.145, f32[512]{0:T(512)S(1)} %bitcast.139, f32[512]{0:T(512)S(1)} %bitcast.142, f32[512]{0:T(512)S(1)} %copy-done.39, f32[]{:T(128)S(6)} %sqrt.8, f32[512,512]{1,0:T(8,128)S(1)} %copy-done.7, f32[]{:T(128)S(6)} %sqrt.7), kind=kOutput, calls=%fused_computation.6 | convolution fusion | flops 1614282752 | bytes 3153928 | tf_op jit(solution)/shard_map/dot_general | solution.py:30
  181.5 1.9 convolution_add_fusion.1
  183.4 2.0 fusion.16
  185.4 1.9 fusion
  187.3 3.6 %multiply_reduce_fusion = (f32[]{:T(128)}, f32[512,512]{1,0:T(8,128)}) fusion(f32[]{:T(128)S(6)} %sqrt.7, f32[512,512]{1,0:T(8,128)S(1)} %copy-done.7, f32[512,512]{1,0:T(8,128)S(1)} %fusion, f32[512,512]{1,0:T(8,128)S(1)} %fusion.16), kind=kOutput, calls=%fused_computation.31 | convolution fusion | flops 1614282752 | bytes 4194312 | tf_op jit(solution)/shard_map/dot_general | solution.py:30
  191.5 1.8 divide_add_fusion
  193.2 1.3 copy.10
  194.6 1.4 fusion.94
  203.1 3.2 %collective-permute-start.5 = (f32[128,1,128]{2,1,0:T(1,128)S(1)}, f32[128,1,128]{2,1,0:T(1,128)S(1)}, u32[]{:S(2)}, u32[]{:S(2)}) collective-permute-start(f32[128,1,128]{2,1,0:T(1,128)S(1)} %get-tuple-element.29), channel_id=1, source_target_pairs={{0,4},{4,8},{8,12},{12,16},{16,20},{20,24},{24,28},{1,5},{5,9},{9,... | collective-permute-start | bytes 196616 | tf_op jit(solution)/shard_map/ppermute | solution.py:17
  206.3 1.3 collective-permute-start.4
  208.2 4.3 %collective-permute-done.4 = f32[128,1,128]{2,1,0:T(1,128)S(1)} collective-permute-done((f32[128,1,128]{2,1,0:T(1,128)S(1)}, f32[128,1,128]{2,1,0:T(1,128)S(1)}, u32[]{:S(2)}, u32[]{:S(2)}) %collective-permute-start.4) | collective-permute-done | bytes 65568 | tf_op jit(solution)/shard_map/ppermute | solution.py:20
  214.4 4.3 %collective-permute-start.7 = (f32[128,1,128]{2,1,0:T(1,128)S(1)}, f32[128,1,128]{2,1,0:T(1,128)S(1)}, u32[]{:S(2)}, u32[]{:S(2)}) collective-permute-start(f32[128,1,128]{2,1,0:T(1,128)S(1)} %get-tuple-element.27), channel_id=1, source_target_pairs={{0,4},{4,8},{8,12},{12,16},{16,20},{20,24},{24,28},{1,5},{5,9},{9,... | collective-permute-start | bytes 196616 | tf_op jit(solution)/shard_map/ppermute | solution.py:17
  220.0 6.1 %psum.39 = f32[2048]{0:T(1024)S(1)} all-reduce(f32[2048]{0:T(1024)S(1)} %bitcast.133), channel_id=1, replica_groups=mesh['space'=8,'mem'=4] {'mem'}, use_global_device_ids=true, to_apply=%region_23.0 | all-reduce | flops 2048 | bytes 16384 | tf_op jit(solution)/shard_map/psum | solution.py:92
  (179 shorter events, 31.3 us)
Async XLA Ops:
  7.2 8.2 %copy-start.25 = (f32[128,4,128]{2,1,0:T(4,128)S(1)}, f32[128,4,128]{2,1,0:T(4,128)}, u32[]{:S(2)}) copy-start(f32[128,4,128]{2,1,0:T(4,128)} %param.13) | copy-start | bytes 786436
  7.2 39.4 %all-gather.7.cloned.1.call-start = ((), (), s32[]{:S(2)}) async-start(), calls=%async_computation.1 | async-start | bytes 1310720 | tf_op jit(solution)/shard_map/all_gather | solution.py:132
  7.9 12.9 %copy-start.31 = (f32[1,4,128]{2,1,0:T(4,128)}, f32[1,4,128]{2,1,0:T(4,128)S(1)}, u32[]{:S(2)}) copy-start(f32[1,4,128]{2,1,0:T(4,128)S(1)} %get-tuple-element.46) | copy-start | bytes 6148
  7.9 24.1 %copy-start.29 = (f32[4,128]{1,0:T(4,128)}, f32[4,128]{1,0:T(4,128)S(1)}, u32[]{:S(2)}) copy-start(f32[4,128]{1,0:T(4,128)S(1)} %get-tuple-element.45) | copy-start | bytes 6148
  9.2 8.1 %collective-permute-start = (f32[133,1,128]{2,1,0:T(1,128)S(1)}, f32[133,1,128]{2,1,0:T(1,128)S(1)}, u32[]{:S(2)}, u32[]{:S(2)}) collective-permute-start(f32[133,1,128]{2,1,0:T(1,128)S(1)} %get-tuple-element.23), channel_id=1, source_target_pairs={{0,4},{4,8},{8,12},{12,16},{16,20},{20,24},{24,28},{1,5},{5,9},{9,... | collective-permute-start | bytes 204296 | tf_op jit(solution)/shard_map/ppermute | solution.py:17
  14.1 6.2 %collective-permute-start.1 = (f32[133,1,128]{2,1,0:T(1,128)S(1)}, f32[133,1,128]{2,1,0:T(1,128)S(1)}, u32[]{:S(2)}, u32[]{:S(2)}) collective-permute-start(f32[133,1,128]{2,1,0:T(1,128)S(1)} %get-tuple-element.22), channel_id=1, source_target_pairs={{4,0},{8,4},{12,8},{16,12},{20,16},{24,20},{28,24},{5,1},{9,5},{13... | collective-permute-start | bytes 204296 | tf_op jit(solution)/shard_map/ppermute | solution.py:20
  16.1 106.7 %all-reduce.11.cloned.1.call-start = ((), (), s32[]{:S(2)}) async-start(), calls=%async_computation.3 | async-start | bytes 1048576 | tf_op jit(solution)/shard_map/psum | solution.py:139
  20.9 11.1 %copy-start.27 = (f32[4,128]{1,0:T(4,128)}, f32[4,128]{1,0:T(4,128)S(1)}, u32[]{:S(2)}) copy-start(f32[4,128]{1,0:T(4,128)S(1)} %get-tuple-element.41) | copy-start | bytes 6148
  21.4 10.6 %copy-start.2 = (f32[128,4,128]{2,1,0:T(4,128)}, f32[128,4,128]{2,1,0:T(4,128)S(1)}, u32[]{:S(2)}) copy-start(f32[128,4,128]{2,1,0:T(4,128)S(1)} %add_multiply_fusion.1) | copy-start | bytes 786436
  21.5 6.2 %collective-permute-start.2 = (f32[128,1,128]{2,1,0:T(1,128)S(1)}, f32[128,1,128]{2,1,0:T(1,128)S(1)}, u32[]{:S(2)}, u32[]{:S(2)}) collective-permute-start(f32[128,1,128]{2,1,0:T(1,128)S(1)} %get-tuple-element.35), channel_id=1, source_target_pairs={{0,4},{4,8},{8,12},{12,16},{16,20},{20,24},{24,28},{1,5},{5,9},{9,... | collective-permute-start | bytes 196616 | tf_op jit(solution)/shard_map/ppermute | solution.py:17
  25.8 6.2 %collective-permute-start.3 = (f32[128,1,128]{2,1,0:T(1,128)S(1)}, f32[128,1,128]{2,1,0:T(1,128)S(1)}, u32[]{:S(2)}, u32[]{:S(2)}) collective-permute-start(f32[128,1,128]{2,1,0:T(1,128)S(1)} %get-tuple-element.34), channel_id=1, source_target_pairs={{4,0},{8,4},{12,8},{16,12},{20,16},{24,20},{28,24},{5,1},{9,5},{13... | collective-permute-start | bytes 196616 | tf_op jit(solution)/shard_map/ppermute | solution.py:20
  27.3 5.2 %copy-start.13 = (f32[128,4,127]{2,1,0:T(4,128)}, f32[128,4,127]{2,1,0:T(4,128)S(1)}, u32[]{:S(2)}) copy-start(f32[128,4,127]{2,1,0:T(4,128)S(1)} %get-tuple-element.32) | copy-start | bytes 780292
  27.3 5.2 %copy-start.15 = (f32[128,4,127]{2,1,0:T(4,128)}, f32[128,4,127]{2,1,0:T(4,128)S(1)}, u32[]{:S(2)}) copy-start(f32[128,4,127]{2,1,0:T(4,128)S(1)} %get-tuple-element.33) | copy-start | bytes 780292
  27.7 4.8 %copy-start.21 = (f32[128,1,128]{2,1,0:T(1,128)}, f32[128,1,128]{2,1,0:T(1,128)S(1)}, u32[]{:S(2)}) copy-start(f32[128,1,128]{2,1,0:T(1,128)S(1)} %collective-permute-done.2) | copy-start | bytes 196612
  33.7 5.7 %copy-start.19 = (f32[128,128]{1,0:T(8,128)}, f32[128,128]{1,0:T(8,128)S(1)}, u32[]{:S(2)}) copy-start(f32[128,128]{1,0:T(8,128)S(1)} %get-tuple-element.48) | copy-start | bytes 196612
  33.7 5.7 %copy-start.47 = (f32[128]{0:T(128)S(1)}, f32[128]{0:T(128)}, u32[]{:S(2)}) copy-start(f32[128]{0:T(128)} %param.12) | copy-start | bytes 1540
  33.7 5.7 %copy-start.57 = (f32[128]{0:T(128)S(1)}, f32[128]{0:T(128)}, u32[]{:S(2)}) copy-start(f32[128]{0:T(128)} %param.11) | copy-start | bytes 1540
  39.4 84.7 %copy-start.50 = (f32[128]{0:T(128)}, f32[128]{0:T(128)S(1)}, u32[]{:S(2)}) copy-start(f32[128]{0:T(128)S(1)} %get-tuple-element.43) | copy-start | bytes 1540
  45.4 122.7 %copy-start.4 = (f32[512,128]{1,0:T(8,128)}, f32[512,128]{1,0:T(8,128)S(1)}, u32[]{:S(2)}) copy-start(f32[512,128]{1,0:T(8,128)S(1)} %all_gather.15) | copy-start | bytes 786436
  46.5 102.7 %copy-start = (f32[512,512]{1,0:T(8,128)S(1)}, f32[512,512]{1,0:T(8,128)}, u32[]{:S(2)}) copy-start(f32[512,512]{1,0:T(8,128)} %all-gather.7.cloned.1.call-done) | copy-start | bytes 3145732
  49.7 100.2 %all-gather.5.cloned.1.call-start = ((), (), s32[]{:S(2)}) async-start(), calls=%async_computation | async-start | bytes 1310720 | tf_op jit(solution)/shard_map/all_gather | solution.py:141
  122.9 35.8 %all-gather.9.cloned.1.call-start = ((), (), s32[]{:S(2)}) async-start(), calls=%async_computation.2 | async-start | bytes 1310720 | tf_op jit(solution)/shard_map/all_gather | solution.py:143
  149.2 15.3 %copy-start.45 = (f32[4,1,128]{2,1,0:T(1,128)}, f32[4,1,128]{2,1,0:T(1,128)S(1)}, u32[]{:S(2)}) copy-start(f32[4,1,128]{2,1,0:T(1,128)S(1)} %all-gather) | copy-start | bytes 6148
  203.1 4.6 %copy-start.36 = (f32[4,127]{1,0:T(4,128)S(1)}, f32[4,127]{1,0:T(4,128)}, u32[]{:S(2)}) copy-start(f32[4,127]{1,0:T(4,128)} %slice.189) | copy-start | bytes 6100
  203.1 5.1 %collective-permute-start.5 = (f32[128,1,128]{2,1,0:T(1,128)S(1)}, f32[128,1,128]{2,1,0:T(1,128)S(1)}, u32[]{:S(2)}, u32[]{:S(2)}) collective-permute-start(f32[128,1,128]{2,1,0:T(1,128)S(1)} %get-tuple-element.29), channel_id=1, source_target_pairs={{0,4},{4,8},{8,12},{12,16},{16,20},{20,24},{24,28},{1,5},{5,9},{9,... | collective-permute-start | bytes 196616 | tf_op jit(solution)/shard_map/ppermute | solution.py:17
  206.3 6.2 %collective-permute-start.4 = (f32[128,1,128]{2,1,0:T(1,128)S(1)}, f32[128,1,128]{2,1,0:T(1,128)S(1)}, u32[]{:S(2)}, u32[]{:S(2)}) collective-permute-start(f32[128,1,128]{2,1,0:T(1,128)S(1)} %get-tuple-element.28), channel_id=1, source_target_pairs={{4,0},{8,4},{12,8},{16,12},{20,16},{24,20},{28,24},{5,1},{9,5},{13... | collective-permute-start | bytes 196616 | tf_op jit(solution)/shard_map/ppermute | solution.py:20
  207.7 4.8 %copy-start.10 = (f32[128,4,127]{2,1,0:T(4,128)S(1)}, f32[128,4,127]{2,1,0:T(4,128)}, u32[]{:S(2)}) copy-start(f32[128,4,127]{2,1,0:T(4,128)} %copy-done.9) | copy-start | bytes 780292
  207.7 4.8 %copy-start.12 = (f32[128,4,127]{2,1,0:T(4,128)S(1)}, f32[128,4,127]{2,1,0:T(4,128)}, u32[]{:S(2)}) copy-start(f32[128,4,127]{2,1,0:T(4,128)} %copy-done.11) | copy-start | bytes 780292
  207.7 4.8 %copy-start.34 = (f32[4,128]{1,0:T(4,128)S(1)}, f32[4,128]{1,0:T(4,128)}, u32[]{:S(2)}) copy-start(f32[4,128]{1,0:T(4,128)} %get-tuple-element.21) | copy-start | bytes 6148
  207.7 4.8 %copy-start.35 = (f32[4,128]{1,0:T(4,128)S(1)}, f32[4,128]{1,0:T(4,128)}, u32[]{:S(2)}) copy-start(f32[4,128]{1,0:T(4,128)} %get-tuple-element.38) | copy-start | bytes 6148
  214.4 12.4 %collective-permute-start.7 = (f32[128,1,128]{2,1,0:T(1,128)S(1)}, f32[128,1,128]{2,1,0:T(1,128)S(1)}, u32[]{:S(2)}, u32[]{:S(2)}) collective-permute-start(f32[128,1,128]{2,1,0:T(1,128)S(1)} %get-tuple-element.27), channel_id=1, source_target_pairs={{0,4},{4,8},{8,12},{12,16},{16,20},{20,24},{24,28},{1,5},{5,9},{9,... | collective-permute-start | bytes 196616 | tf_op jit(solution)/shard_map/ppermute | solution.py:17
  218.7 8.1 %collective-permute-start.6 = (f32[128,1,128]{2,1,0:T(1,128)S(1)}, f32[128,1,128]{2,1,0:T(1,128)S(1)}, u32[]{:S(2)}, u32[]{:S(2)}) collective-permute-start(f32[128,1,128]{2,1,0:T(1,128)S(1)} %get-tuple-element.26), channel_id=1, source_target_pairs={{4,0},{8,4},{12,8},{16,12},{20,16},{24,20},{28,24},{5,1},{9,5},{13... | collective-permute-start | bytes 196616 | tf_op jit(solution)/shard_map/ppermute | solution.py:20
  (39 other events, 70.2 us)
Sparse Core Ops, SparseCore 0:
  16.2 19.0 all-gather.6
  49.8 72.9 all-reduce.10
  124.4 15.8 all-gather.4
  141.8 16.6 all-gather.8
where the time goes:
time: 235 us; the launch traced here: 234 us
  waiting for transfers between devices  85.9 us (37%)
  blocking collectives  42.7 us (18%)
  matrix products  37 us (16%)
  starting transfers between devices  22.1 us (9%)
  other arithmetic  19 us (8%)
  between operations  16.4 us (7%)
  local copies, waits for them, and re-layouts  11.4 us (5%)
    psum x1, waiting for transfers between devices, local(): lax.psum((gram_rows, pull_rows, cross_rows), 'space')  73.1 us
    dot_general x11, matrix products, contract(): lax.dot_general(left_side, right_side, (((left_dim,), (right_dim,)), ((),...  20.7 us
    psum x1, blocking collectives, local(): lax.psum((gram_rows, pull_rows, cross_rows), 'space')  19.7 us
    ppermute x4, starting transfers between devices, extended_2(): lax.ppermute(lax.slice_in_dim(block, block.shape[dim] - width, None, axis...  16.7 us
    dot_general x12, matrix products, matmul(): jnp.dot(left_side, right_side, precision=highest, preferred_element_type=...  16.4 us
    psum x2, blocking collectives, member_total(): return lax.psum(vector, 'mem')  11.8 us
    ppermute x4, waiting for transfers between devices, extended_2(): lax.ppermute(lax.slice_in_dim(block, 0, width, axis=dim), axis, backward)  11.5 us
    unnamed x119, local copies, waits for them, and re-layouts  7.33 us
  transfers between devices with their start and end apart: 12, of which 6 were waited for; matrix products, arithmetic and copies ran while one was open for 6% of the time, Pallas kernels for 0%

commit v1 on v0

v1 whole, which is shorter than its diff:
```python
import functools
import jax
import jax.numpy as jnp
from jax import lax
from jax.experimental import pallas as pl
from jax.experimental.pallas import tpu as pltpu
from jax.sharding import PartitionSpec as P

MESH = pl.DeviceIdType.MESH
HIGH = lax.Precision.HIGH
HIGHEST = lax.Precision.HIGHEST
VMEM_SPEC = pl.BlockSpec(memory_space=pltpu.VMEM)


def dot(a, b, a_dims, b_dims, precision=HIGH):
    return lax.dot_general(
        a, b, ((a_dims, b_dims), ((), ())), precision=precision, preferred_element_type=jnp.float32
    )


def mm(a, b):
    return dot(a, b, (1,), (0,))


def remote(src, dst, send, recv, s, m):
    return pltpu.make_async_remote_copy(
        src_ref=src, dst_ref=dst, send_sem=send, recv_sem=recv, device_id=(s, m), device_id_type=MESH
    )


def params(ident):
    return pltpu.CompilerParams(collective_id=ident, has_side_effects=True)


def halo_body(n_space, last, first, low, high, send, recv):
    s, m = lax.axis_index("space"), lax.axis_index("mem")
    barrier = pltpu.get_barrier_semaphore()
    has_low, has_high = s > 0, s < n_space - 1

    @pl.when(has_low)
    def _():
        pl.semaphore_signal(barrier, inc=1, device_id=(s - 1, m), device_id_type=MESH)

    @pl.when(has_high)
    def _():
        pl.semaphore_signal(barrier, inc=1, device_id=(s + 1, m), device_id_type=MESH)

    pl.semaphore_wait(barrier, has_low.astype(jnp.int32) + has_high.astype(jnp.int32))

    up = remote(last, low, send.at[0], recv.at[0], s + 1, m)
    down = remote(first, high, send.at[1], recv.at[1], s - 1, m)

    @pl.when(has_high)
    def _():
        up.start()

    @pl.when(has_low)
    def _():
        down.start()

    def finish():
        @pl.when(has_low)
        def _():
            up.wait_recv()
            down.wait_send()

        @pl.when(has_high)
        def _():
            down.wait_recv()
            up.wait_send()

    return finish


def halo(n_space, last, first, ident):
    def body(last_ref, first_ref, low, high, send, recv):
        halo_body(n_space, last_ref, first_ref, low, high, send, recv)()

    shape = jax.ShapeDtypeStruct(last.shape, last.dtype)
    low, high = pl.pallas_call(
        body,
        out_shape=(shape, shape),
        in_specs=[VMEM_SPEC] * 2,
        out_specs=(VMEM_SPEC,) * 2,
        scratch_shapes=[pltpu.SemaphoreType.DMA((2,)), pltpu.SemaphoreType.DMA((2,))],
        compiler_params=params(ident),
        name="halo",
    )(last, first)
    s = lax.axis_index("space")
    return jnp.where(s > 0, low, 0.0), jnp.where(s < n_space - 1, high, 0.0)


def gather_members(n_mem, arrays, dims, ident):
    count = len(arrays)

    def body(*refs):
        ins, outs = refs[:count], refs[count : 2 * count]
        send, recv, own = refs[2 * count :]
        s, m = lax.axis_index("space"), lax.axis_index("mem")
        barrier = pltpu.get_barrier_semaphore()
        for k in range(1, n_mem):
            pl.semaphore_signal(
                barrier, inc=1, device_id=(s, lax.rem(m + k, n_mem)), device_id_type=MESH
            )

        def part(i, which):
            width = arrays[i].shape[dims[i]]
            where = [slice(None)] * arrays[i].ndim
            where[dims[i]] = pl.ds(pl.multiple_of(which * width, width), width)
            return outs[i].at[tuple(where)]

        mine = [pltpu.make_async_copy(ins[i], part(i, m), own.at[i]) for i in range(count)]
        for copy in mine:
            copy.start()
        pl.semaphore_wait(barrier, n_mem - 1)
        copies = []
        for k in range(1, n_mem):
            for i in range(count):
                copy = remote(
                    ins[i], part(i, m), send.at[i, k], recv.at[i, k], s, lax.rem(m + k, n_mem)
                )
                copy.start()
                copies.append(copy)
        for copy in copies:
            copy.wait()
        for copy in mine:
            copy.wait()

    shapes = []
    for array, dim in zip(arrays, dims):
        shape = list(array.shape)
        shape[dim] *= n_mem
        shapes.append(jax.ShapeDtypeStruct(tuple(shape), array.dtype))
    return pl.pallas_call(
        body,
        out_shape=tuple(shapes),
        in_specs=[VMEM_SPEC] * count,
        out_specs=(VMEM_SPEC,) * count,
        scratch_shapes=[
            pltpu.SemaphoreType.DMA((count, n_mem)),
            pltpu.SemaphoreType.DMA((count, n_mem)),
            pltpu.SemaphoreType.DMA((count,)),
        ],
        compiler_params=params(ident),
        name="gather_members",
    )(*arrays)


def reduce_gather(n_space, n_mem, rows, ident):
    pieces, height, width = rows.shape
    near = 2 if n_space % 2 == 0 else 1
    far = n_space // near
    half = 2 if n_mem % 2 == 0 else 1
    wide = n_mem // half
    group = max(1, far // 4)
    groups = far // group

    def body(x, out, buf, rs_send, rs_recv, own, a_send, a_recv, b_send, b_recv, p_send, p_recv, q_send, q_recv):
        s, m = lax.axis_index("space"), lax.axis_index("mem")
        a, b = s // near, lax.rem(s, near)
        p, q = m // half, lax.rem(m, half)
        barrier = pltpu.get_barrier_semaphore()
        peers = [(lax.rem(s + k, n_space), m) for k in range(1, n_space)]
        peers += [(s, lax.rem(p + k, wide) * half + q) for k in range(1, wide)]
        peers += [(s, p * half + lax.rem(q + k, half)) for k in range(1, half)]
        for peer in peers:
            pl.semaphore_signal(barrier, inc=1, device_id=peer, device_id_type=MESH)
        mine = pltpu.make_async_copy(x.at[s], buf.at[s], own.at[0])
        mine.start()
        pl.semaphore_wait(barrier, len(peers))
        scatter = []
        for k in range(1, n_space):
            to = lax.rem(s + k, n_space)
            copy = remote(x.at[to], buf.at[s], rs_send.at[k], rs_recv.at[k], to, m)
            copy.start()
            scatter.append(copy)
        mine.wait()
        for copy in scatter:
            copy.wait_recv()
        total = buf[0]
        for k in range(1, n_space):
            total = total + buf[k]
        out[m, b, a] = total

        waits = list(scatter)
        stage_a = []
        for k in range(1, far):
            to = lax.rem(a + k, far)
            copy = remote(
                out.at[m, b, a], out.at[m, b, a], a_send.at[k], a_recv.at[k], to * near + b, m
            )
            copy.start()
            stage_a.append(copy)
        if group == 1:
            a_steps = [([], a)] + [([stage_a[k - 1]], lax.rem(a + far - k, far)) for k in range(1, far)]
        else:
            a_steps = [(stage_a if g == 0 else [], g * group) for g in range(groups)]
        steps_b = []
        for index, (needs, start) in enumerate(a_steps):
            for copy in needs:
                copy.wait_recv()
            steps_b.append((start, index))
            flow(
                out, s, m, b, p, q, start, index, 0, group, near, half, wide,
                b_send, b_recv, p_send, p_recv, q_send, q_recv, waits,
            )
        waits += stage_a
        for start, index in steps_b:
            pend = []
            for kb in range(1, near):
                pend.append((start, index, kb))
            for start_, index_, kb in pend:
                from_b = lax.rem(b + near - kb, near)
                piece = out.at[m, from_b, pl.ds(start_, group)]
                remote(piece, piece, b_send.at[kb, index_], b_recv.at[kb, index_], s, m).wait_recv()
                flow(
                    out, s, m, from_b, p, q, start_, index_, kb, group, near, half, wide,
                    None, None, p_send, p_recv, q_send, q_recv, waits,
                )
        for start, index in steps_b:
            for kb in range(near):
                which_b = lax.rem(b + near - kb, near)
                for kp in range(1, wide):
                    from_p = lax.rem(p + wide - kp, wide)
                    piece = out.at[from_p * half + q, which_b, pl.ds(start, group)]
                    remote(
                        piece, piece, p_send.at[kp, kb, index], p_recv.at[kp, kb, index], s, m
                    ).wait_recv()
                    for kq in range(1, half):
                        to_q = lax.rem(q + kq, half)
                        copy = remote(
                            piece, piece, q_send.at[kq, kp, kb, index], q_recv.at[kq, kp, kb, index],
                            s, p * half + to_q,
                        )
                        copy.start()
                        waits.append(copy)
        for start, index in steps_b:
            for kb in range(near):
                which_b = lax.rem(b + near - kb, near)
                for kp in range(wide):
                    from_p = lax.rem(p + wide - kp, wide)
                    for kq in range(1, half):
                        from_q = lax.rem(q + half - kq, half)
                        piece = out.at[from_p * half + from_q, which_b, pl.ds(start, group)]
                        remote(
                            piece, piece, q_send.at[kq, kp, kb, index],
                            q_recv.at[kq, kp, kb, index], s, m,
                        ).wait_recv()
        for copy in waits:
            copy.wait_send()

    def flow(
        out, s, m, which_b, p, q, start, index, kb, group, near, half, wide,
        b_send, b_recv, p_send, p_recv, q_send, q_recv, waits,
    ):
        piece = out.at[m, which_b, pl.ds(start, group)]
        for kp in range(1, wide):
            copy = remote(
                piece, piece, p_send.at[kp, kb, index], p_recv.at[kp, kb, index],
                s, lax.rem(p + kp, wide) * half + q,
            )
            copy.start()
            waits.append(copy)
        if b_send is not None:
            for k in range(1, near):
                to = (s // near) * near + lax.rem(which_b + k, near)
                copy = remote(piece, piece, b_send.at[k, index], b_recv.at[k, index], to, m)
                copy.start()
                waits.append(copy)
        for kq in range(1, half):
            copy = remote(
                piece, piece, q_send.at[kq, 0, kb, index], q_recv.at[kq, 0, kb, index],
                s, p * half + lax.rem(q + kq, half),
            )
            copy.start()
            waits.append(copy)

    dma = pltpu.SemaphoreType.DMA
    out = pl.pallas_call(
        body,
        out_shape=jax.ShapeDtypeStruct((n_mem, near, far, height, width), rows.dtype),
        in_specs=[VMEM_SPEC],
        out_specs=VMEM_SPEC,
        scratch_shapes=[
            pltpu.VMEM(rows.shape, rows.dtype),
            dma((n_space,)), dma((n_space,)), dma((1,)),
            dma((far,)), dma((far,)),
            dma((near, groups)), dma((near, groups)),
            dma((wide, near, groups)), dma((wide, near, groups)),
            dma((half, wide, near, groups)), dma((half, wide, near, groups)),
        ],
        compiler_params=params(ident),
        name="reduce_gather",
    )(rows)
    return out


def neighbours(ext):
    center, north, south = ext[1:-1], ext[:-2], ext[2:]
    border = jnp.zeros_like(center[..., :1])
    west = jnp.concatenate([border, center[..., :-1]], axis=-1)
    east = jnp.concatenate([center[..., 1:], border], axis=-1)
    return center, north, south, west, east


def substep(ext, coef, sea):
    center, north, south, west, east = neighbours(ext)
    return sea * (
        center
        + coef[0] * (north - center)
        + coef[1] * (south - center)
        + coef[2] * (west - center)
        + coef[3] * (east - center)
    )


def transpose_step(ext, coef_ext):
    center = ext[1:-1]
    inner = coef_ext[:, 1:-1]
    from_south = coef_ext[0, 2:] * ext[2:]
    from_north = coef_ext[1, :-2] * ext[:-2]
    border = jnp.zeros_like(center[..., :1])
    from_east = jnp.concatenate([(inner[2] * center)[..., 1:], border], axis=-1)
    from_west = jnp.concatenate([border, (inner[3] * center)[..., :-1]], axis=-1)
    keeping = 1.0 - inner[0] - inner[1] - inner[2] - inner[3]
    return center * keeping + from_south + from_north + from_east + from_west


def coef_terms(weight, ext):
    center, north, south, west, east = neighbours(ext)
    return jnp.stack(
        [jnp.sum(weight * (side - center), axis=1) for side in (north, south, west, east)]
    )


def local(n_space, n_mem, prior, stencil, sea_mask, sites, data, precision, cotangent):
    members, rows, cols = prior.shape
    total = members * n_mem
    scale = jnp.sqrt(jnp.float32(total - 1))
    m = lax.axis_index("mem")
    prior_t = jnp.transpose(prior, (1, 0, 2))
    cot_t = jnp.transpose(cotangent, (1, 0, 2))
    aux = jnp.concatenate(
        [
            jnp.transpose(stencil, (1, 0, 2)),
            sea_mask.astype(jnp.float32)[:, None],
            jnp.zeros((rows, 3, cols), jnp.float32),
        ],
        axis=1,
    )
    packed = jnp.concatenate([prior_t, aux], axis=1)
    low, high = halo(n_space, packed[-2:], packed[:2], 1)
    (cot_full,) = gather_members(n_mem, [cot_t], [1], 2)
    ext = jnp.concatenate([low, packed, high], axis=0)
    prior_ext = ext[:, :members]
    coef_ext = jnp.transpose(ext[:, members : members + 4], (1, 0, 2))[:, :, None]
    sea_ext = ext[:, members + 4][:, None]
    first_ext = substep(prior_ext, coef_ext[:, 1:-1], sea_ext[1:-1])
    state = substep(first_ext, coef_ext[:, 2:-2], sea_ext[2:-2])
    cells = jnp.arange(rows * cols, dtype=jnp.int32).reshape(rows, 1, cols)
    onehot = (sites[0][None, :, None] == cells).astype(jnp.float32)
    picked = dot(state, onehot, (0, 2), (0, 2), HIGHEST)
    tanh_picked = jnp.tanh(picked)
    observed = picked + 0.5 * tanh_picked
    sums = jnp.sum(state, axis=1)
    sums = jnp.concatenate([sums, jnp.zeros((-rows % 8, cols), jnp.float32)], axis=0)[None]
    obs_full, all_sums = gather_members(n_mem, [observed, sums], [0, 0], 3)
    average = jnp.sum(all_sums, axis=0)[:rows] / total
    observed_mean = jnp.sum(obs_full, axis=0) / total
    deviations = (state - average[:, None]) / scale
    anom_full = (obs_full - observed_mean) * precision / scale
    obs_anom = (observed - observed_mean) * precision / scale
    innovation = precision * (data - observed_mean)
    gram_rows = dot(obs_anom, anom_full, (1,), (1,))
    cross_rows = dot(deviations, cot_full, (0, 2), (0, 2))
    pull_rows = jnp.sum(obs_anom * innovation, axis=1)
    block = jnp.concatenate(
        [gram_rows, cross_rows, jnp.broadcast_to(pull_rows[:, None], (members, 128))], axis=1
    )
    near = 2 if n_space % 2 == 0 else 1
    block = block.reshape(n_space, members // n_space, -1)
    done = reduce_gather(n_space, n_mem, block, 4)
    done = jnp.transpose(done, (0, 2, 1, 3, 4)).reshape(total, -1)
    gram, cross, pull = done[:, :total], done[:, total : 2 * total], done[:, 2 * total]

    identity = jnp.eye(total, dtype=jnp.float32)
    system = identity + gram
    norm = jnp.sqrt(jnp.sum(system * system))
    root = jnp.sqrt(norm)
    approach = system / norm
    factor = 1.5 * identity - 0.5 * approach
    square = mm(factor, factor)
    transform = (1.5 * factor + mm(square, square - 1.5 * factor)) / root
    mid_pull = jnp.sum(transform * pull[None, :], axis=1)
    mean_weights = jnp.sum(transform * mid_pull[None, :], axis=1)
    mean_bar = jnp.sum(cross, axis=1)
    mid_bar = jnp.sum(transform * mean_bar[None, :], axis=1)
    pull_bar = jnp.sum(transform * mid_bar[None, :], axis=1)
    half_weight = (
        scale * cross + mean_bar[:, None] * mid_pull[None, :] + mid_bar[:, None] * pull[None, :]
    )
    weight_bar = 0.5 * (half_weight + half_weight.T)
    polar_bar = weight_bar / root
    scale_bar = -0.5 * jnp.sum(weight_bar * transform) / norm
    bar_square = mm(polar_bar, square)
    bar_mixed = mm(polar_bar, 2.0 * square - 1.5 * factor)
    square_bar = 0.5 * (bar_mixed + bar_mixed.T)
    bar_factor = mm(square_bar, factor)
    half_bar = 0.75 * polar_bar - 1.5 * 0.5 * bar_square + bar_factor
    approach_bar = -0.5 * (half_bar + half_bar.T)
    scale_bar = scale_bar - jnp.sum(approach_bar * approach) / norm
    sym_bar = 2.0 * (approach_bar + scale_bar * system) / norm

    offset = m * members
    take = lambda x: lax.dynamic_slice_in_dim(x, offset, members, 0)
    mix_rows = take(transform) + take(mean_weights)[:, None] / scale
    row_weights = jnp.sum(transform, axis=0) + jnp.sum(mean_weights) / scale
    mix_rows = mix_rows + ((1.0 - row_weights) / total)[None, :]
    sym_rows = take(sym_bar) - (jnp.sum(sym_bar, axis=0) / total)[None, :]
    sym_rows = sym_rows - (scale / total * pull_bar)[None, :]
    observed_bar = (precision / scale) * (
        mm(sym_rows, anom_full)
        + (take(pull_bar) - jnp.sum(pull_bar) / total)[:, None] * innovation[None, :]
    )
    picked_bar = observed_bar * (1.0 + 0.5 * (1.0 - tanh_picked * tanh_picked))
    field_bar = jnp.stack(
        [mm(mix_rows, cot_full[r]) + mm(picked_bar, onehot[r]) for r in range(rows)]
    )
    second_bar = sea_ext[2:-2] * field_bar
    low_bar, high_bar = halo(n_space, second_bar[-2:], second_bar[:2], 5)
    bar_ext = jnp.concatenate([low_bar, second_bar, high_bar], axis=0)
    first_bar = sea_ext[1:-1] * transpose_step(bar_ext, coef_ext)
    coef_part = coef_terms(second_bar, first_ext) + coef_terms(first_bar[1:-1], prior_ext[1:-1])
    (coef_all,) = gather_members(n_mem, [coef_part.reshape(1, 4 * rows, cols)], [0], 6)
    prior_grad = transpose_step(first_bar, coef_ext[:, 1:-1])
    coef_total = jnp.sum(coef_all, axis=0).reshape(4, rows, cols)
    return (
        jnp.transpose(prior_grad, (1, 0, 2)),
        coef_total / jnp.sqrt(jnp.float32(total)),
    )


def solution(mesh):
    placed = (
        P("mem", "space", None),
        P(None, "space", None),
        P("space", None),
        P("space", None),
        P("space"),
        P("space"),
        P("mem", "space", None),
    )
    return jax.shard_map(
        functools.partial(local, mesh.shape["space"], mesh.shape["mem"]),
        mesh=mesh,
        in_specs=placed,
        out_specs=(P("mem", "space", None), P(None, "space", None)),
        check_vma=False,
    )
```

time: 235 us -> 170 us (0.72)
  Pallas kernels: 0 us -> 89.2 us
  waiting for transfers between devices: 85.9 us -> 0 us
  blocking collectives: 42.7 us -> 0 us
  starting transfers between devices: 22.1 us -> 0 us
  between operations: 16.4 us -> 4.55 us
  local copies, waits for them, and re-layouts: 11.4 us -> 23.2 us
  matrix products: 37 us -> 25.3 us
  other arithmetic: 19 us -> 26.1 us
    pallas_call x0 -> x6, Pallas kernels: none -> 89.2 us  [the longest x1 41 us: reduce_gather(): pl.pallas_call(body, out_shape=jax.ShapeDtypeStruct((n_mem, near, far, he...]
    psum x1 -> x0, waiting for transfers between devices: 73.1 us -> none  [local(): lax.psum((gram_rows, pull_rows, cross_rows), 'space')]
    psum x3 -> x0, blocking collectives: 31.5 us -> none  [the longest x1 19.7 us: local(): lax.psum((gram_rows, pull_rows, cross_rows), 'space')]
    ppermute x8 -> x0, starting transfers between devices: 21.9 us -> none  [the longest x4 16.7 us: extended_2(): lax.ppermute(lax.slice_in_dim(block, block.shape[dim] - width, None, axis...]
    ppermute x8 -> x0, waiting for transfers between devices: 12.2 us -> none  [the longest x4 11.5 us: extended_2(): lax.ppermute(lax.slice_in_dim(block, 0, width, axis=dim), axis, backward)]
    dot_general x23 -> x17, matrix products: 37 us -> 25.3 us  [dot(): lax.dot_general(a, b, ((a_dims, b_dims), ((), ())), precision=precision,...]
    all_gather x2 -> x0, blocking collectives: 11.2 us -> none  [the longest x1 5.99 us: local(): lax.all_gather(obs_anom, 'mem', axis=0, tiled=True)]
    reduce_sum x10 -> x13, other arithmetic: 11.5 us -> 17.2 us  [the longest x1 3.49 us: local(): mean_weights = jnp.sum(transform * mid_pull[None, :], axis=1)]
  transfers between devices with their start and end apart: 12 -> 0, of which waited for: 6 -> 0; matrix products, arithmetic and copies ran while one was open for 6% -> 0% of each run, Pallas kernels for 0% -> 0%
where the time goes in v1:
time: 170 us; the launch traced here: 168 us
  Pallas kernels  89.2 us (52%)
  other arithmetic  26.1 us (15%)
  matrix products  25.3 us (15%)
  local copies, waits for them, and re-layouts  23.2 us (14%)
  between operations  4.55 us (3%)
    pallas_call x1, Pallas kernels, reduce_gather(): pl.pallas_call(body, out_shape=jax.ShapeDtypeStruct((n_mem, near, far, he...  41 us
    pallas_call x3, Pallas kernels, gather_members(): pl.pallas_call(body, out_shape=tuple(shapes), in_specs=[VMEM_SPEC] * coun...  27.6 us
    dot_general x17, matrix products, dot(): lax.dot_general(a, b, ((a_dims, b_dims), ((), ())), precision=precision,...  25.3 us
    pallas_call x2, Pallas kernels, halo(): pl.pallas_call(body, out_shape=(shape, shape), in_specs=[VMEM_SPEC] * 2,...  20.6 us
    unnamed x58, local copies, waits for them, and re-layouts  7.49 us
    reduce_sum x1, other arithmetic, local(): mean_weights = jnp.sum(transform * mid_pull[None, :], axis=1)  3.49 us

profile of v1, /device:TPU:0, one launch (start us, length us, event | category | flops | bytes accessed | tf_op | source)
XLA Modules:
  0.0 168.3 jit_solution(7832472562912524661)
XLA Ops:
  2.0 1.4 broadcast_compare_fusion
  3.4 1.7 copy.87
  6.8 10.6 %halo.2 = (f32[2,136,128]{2,1,0:T(8,128)}, f32[2,136,128]{2,1,0:T(8,128)}) custom-call(f32[2,136,128]{2,1,0:T(8,128)} %get-tuple-element.52.last_ref, f32[2,136,128]{2,1,0:T(8,128)} %get-tuple-element.51.first_ref), custom_call_target="tpu_custom_call" | custom-call | tf_op jit(solution)/shard_map/halo/pallas_call | solution.py:80
  19.7 15.4 %gather_members.4 = f32[4,512,128]{2,1,0:T(8,128)} custom-call(f32[4,128,128]{2,1,0:T(8,128)} %bitcast.174), custom_call_target="tpu_custom_call" | custom-call | tf_op jit(solution)/shard_map/gather_members/pallas_call | solution.py:134
  37.5 7.2 %gather_members.3 = (f32[512,128]{1,0:T(8,128)}, f32[4,8,128]{2,1,0:T(8,128)}) custom-call(f32[128,128]{1,0:T(8,128)} %get-tuple-element.74.refs_0_, f32[1,8,128]{2,1,0:T(8,128)} %pad_bitcast_fusion.refs_1_), custom_call_target="tpu_custom_call" | custom-call | tf_op jit(solution)/shard_map/gather_members/pallas_call | solution.py:134
  46.1 1.0 reduce_sum.226
  47.9 1.3 fusion.68
  50.0 41.0 %reduce_gather.1 = f32[4,2,4,16,1152]{4,3,2,1,0:T(8,128)} custom-call(f32[8,16,1152]{2,1,0:T(8,128)} %bitcast.173), custom_call_target="tpu_custom_call" | custom-call | tf_op jit(solution)/shard_map/reduce_gather/pallas_call | solution.py:279
  91.0 1.9 %copy.36 = f32[4,4,2,16,1152]{4,3,2,1,0:T(8,128)S(1)} copy(f32[4,4,2,16,1152]{4,3,1,2,0:T(8,128)} %bitcast.172) | data formatting | bytes 4718592 | tf_op jit(solution)/shard_map/transpose | solution.py:383
  93.1 1.7 slice_reduce_fusion.1
  95.5 2.5 %copy.59 = f32[512,512]{0,1:T(8,128)} copy(f32[512,512]{1,0:T(8,128)} %get-tuple-element.41) | data formatting | bytes 2097152
  98.1 1.1 fusion.41
  99.2 2.3 %multiply_reduce_fusion.2 = (f32[512]{0:T(512)S(1)}, f32[512,512]{1,0:T(8,128)}) fusion(f32[512]{0:T(512)S(1)} %get-tuple-element.18, f32[]{:T(128)S(6)} %sqrt.7, f32[512,512]{1,0:T(8,128)S(1)} %fusion.41, f32[]{:T(128)S(6)} %sqrt.6, f32[512,1152]{1,0:T(8,128)S(1)} %bitcast.161), kind=kOutput, calls=%fused_computation.34 | convolution fusion | flops 810810880 | bytes 5248512 | tf_op jit(solution)/shard_map/dot_general | solution.py:16
  101.4 2.6 %copy.39 = f32[512,512]{0,1:T(8,128)} copy(f32[512,512]{1,0:T(8,128)} %get-tuple-element.77) | data formatting | bytes 2097152 | tf_op jit(solution)/shard_map/div | solution.py:393
  104.0 1.4 multiply_reduce_fusion.3
  105.4 3.5 %multiply_reduce_fusion.8 = (f32[512]{0:T(512)S(1)}, f32[]{:T(128)}, f32[512,512]{0,1:T(8,128)}) fusion(f32[512,512]{0,1:T(8,128)} %copy.39, f32[512]{0:T(512)S(1)} %multiply_reduce_fusion.3, f32[512]{0:T(512)S(1)} %slice_reduce_fusion, f32[512]{0:T(512)S(1)} %get-tuple-element.76, f32[512]{0:T(512)S(1)} %get-tuple-element.18, f32[512,512]{0,1:T(8,128)} %copy.59), kind=kLoop, calls=%fused_computation.42 | loop fusion | flops 2096639 | bytes 3155972 | tf_op jit(solution)/shard_map/reduce_sum | solution.py:395
  109.6 2.5 %copy.41 = f32[512,512]{1,0:T(8,128)} copy(f32[512,512]{0,1:T(8,128)} %get-tuple-element.71) | data formatting | bytes 2097152 | tf_op jit(solution)/shard_map/add | solution.py:400
  112.1 3.0 %multiply_reduce_fusion.5 = (f32[]{:T(128)}, f32[512]{0:T(512)S(1)}, f32[]{:T(128)}, f32[512]{0:T(512)S(1)}) fusion(f32[512,512]{1,0:T(8,128)} %get-tuple-element.77, f32[512]{0:T(512)S(1)} %get-tuple-element.76, f32[512,512]{1,0:T(8,128)} %copy.41, f32[512,512]{0,1:T(8,128)} %get-tuple-element.71), kind=kLoop, calls=%fused_computation.39 | loop fusion | flops 2096126 | bytes 3151880 | tf_op jit(solution)/shard_map/reduce_sum | solution.py:423
  117.7 2.0 %fusion.55 = f32[128,128]{1,0:T(8,128)} fusion(f32[4,512,128]{2,1,0:T(8,128)} %gather_members.4, f32[512,512]{1,0:T(8,128)} %get-tuple-element.77, s32[]{:T(128)S(6)} %select_n.39, f32[512]{0:T(512)S(1)} %subtract_multiply_fusion.2, f32[128]{0:T(128)S(1)} %dynamic-slice_multiply_fusion), kind=kOutput, calls=%fused_computation.100 | convolution fusion | flops 50462720 | bytes 592388 | tf_op jit(solution)/shard_map/dot_general | solution.py:16
  119.6 2.0 %fusion.53 = f32[128,128]{1,0:T(8,128)} fusion(f32[4,512,128]{2,1,0:T(8,128)} %gather_members.4, f32[512,512]{1,0:T(8,128)} %get-tuple-element.77, s32[]{:T(128)S(6)} %select_n.39, f32[512]{0:T(512)S(1)} %subtract_multiply_fusion.2, f32[128]{0:T(128)S(1)} %dynamic-slice_multiply_fusion), kind=kOutput, calls=%fused_computation.98 | convolution fusion | flops 50462720 | bytes 592388 | tf_op jit(solution)/shard_map/dot_general | solution.py:16
  121.6 2.0 %fusion.51 = f32[128,128]{1,0:T(8,128)} fusion(f32[4,512,128]{2,1,0:T(8,128)} %gather_members.4, f32[512,512]{1,0:T(8,128)} %get-tuple-element.77, s32[]{:T(128)S(6)} %select_n.39, f32[512]{0:T(512)S(1)} %subtract_multiply_fusion.2, f32[128]{0:T(128)S(1)} %dynamic-slice_multiply_fusion), kind=kOutput, calls=%fused_computation.96 | convolution fusion | flops 50462720 | bytes 592388 | tf_op jit(solution)/shard_map/dot_general | solution.py:16
  123.5 2.0 %fusion.57 = f32[128,128]{1,0:T(8,128)} fusion(f32[4,512,128]{2,1,0:T(8,128)} %gather_members.4, f32[512,512]{1,0:T(8,128)} %get-tuple-element.77, s32[]{:T(128)S(6)} %select_n.39, f32[512]{0:T(512)S(1)} %subtract_multiply_fusion.2, f32[128]{0:T(128)S(1)} %dynamic-slice_multiply_fusion), kind=kOutput, calls=%fused_computation.102 | convolution fusion | flops 50462720 | bytes 592388 | tf_op jit(solution)/shard_map/dot_general | solution.py:16
  125.5 3.5 %fusion.19 = f32[512,512]{1,0:T(8,128)} fusion(f32[512,512]{1,0:T(8,128)} %copy-done.21, f32[]{:T(128)S(6)} %sqrt.7, f32[512,512]{1,0:T(8,128)S(1)} %copy-done.2, f32[512,512]{0,1:T(8,128)S(1)} %copy-done.1, f32[512,1152]{1,0:T(8,128)S(1)} %bitcast.162, f32[]{:T(128)S(6)} %sqrt.6), kind=kOutput, calls=%fused_computation.30 | convolution fusion | flops 808714240 | bytes 5242888 | tf_op jit(solution)/shard_map/dot_general | solution.py:16
  129.0 2.1 %fusion.8 = f32[512,512]{1,0:T(8,128)} fusion(f32[512,512]{1,0:T(8,128)S(1)} %copy-done.22, f32[]{:T(128)S(6)} %sqrt.7, f32[512,512]{1,0:T(8,128)S(1)} %copy-done.2, f32[512,512]{0,1:T(8,128)S(1)} %copy-done.1), kind=kOutput, calls=%fused_computation.6 | convolution fusion | flops 807665664 | bytes 4194308 | tf_op jit(solution)/shard_map/dot_general | solution.py:16
  131.1 2.5 %copy.42 = f32[512,512]{0,1:T(8,128)} copy(f32[512,512]{1,0:T(8,128)} %fusion.19) | data formatting | bytes 2097152 | tf_op jit(solution)/shard_map/dot_general | solution.py:16
  133.7 3.9 %convolution_add_fusion = f32[512,512]{1,0:T(8,128)} fusion(f32[512,512]{1,0:T(8,128)} %fusion.8, f32[512,512]{1,0:T(8,128)} %fusion.19, f32[512,512]{0,1:T(8,128)} %copy.42, f32[512,1152]{1,0:T(8,128)S(1)} %bitcast.163, f32[]{:T(128)S(6)} %sqrt.6), kind=kOutput, calls=%fused_computation.4 | convolution fusion | flops 807927808 | bytes 5242884 | tf_op jit(solution)/shard_map/dot_general | solution.py:16
  137.6 2.5 %copy.43 = f32[512,512]{0,1:T(8,128)} copy(f32[512,512]{1,0:T(8,128)} %convolution_add_fusion) | data formatting | bytes 2097152 | tf_op jit(solution)/shard_map/add | solution.py:409
  140.1 2.5 %multiply_reduce_fusion = f32[]{:T(128)} fusion(f32[512,512]{1,0:T(8,128)} %convolution_add_fusion, f32[512,512]{0,1:T(8,128)} %copy.43, f32[]{:T(128)S(6)} %sqrt.6, f32[512,1152]{1,0:T(8,128)S(1)} %bitcast.164), kind=kLoop, calls=%fused_computation.28 | loop fusion | flops 2097151 | bytes 3145736 | tf_op jit(solution)/shard_map/reduce_sum | solution.py:411
  143.3 1.9 %fusion.106 = (f32[512]{0:T(512)S(1)}, f32[512,512]{1,0:T(8,128)S(1)}) fusion(f32[]{:T(128)S(6)} %sqrt.6, f32[512,1152]{1,0:T(8,128)S(1)} %bitcast.165, f32[]{:T(128)S(6)} %sub.208, f32[512,512]{1,0:T(8,128)} %convolution_add_fusion, f32[512,512]{0,1:T(8,128)} %copy.43), kind=kLoop, calls=%fused_computation.197 | loop fusion | flops 2620928 | bytes 4196360 | tf_op jit(solution)/shard_map/reduce_sum | solution.py:419
  145.3 1.0 fusion.14
  147.9 10.0 %halo.3 = (f32[2,128,128]{2,1,0:T(8,128)}, f32[2,128,128]{2,1,0:T(8,128)}) custom-call(f32[2,128,128]{2,1,0:T(8,128)} %get-tuple-element.58.last_ref, f32[2,128,128]{2,1,0:T(8,128)} %get-tuple-element.57.first_ref), custom_call_target="tpu_custom_call" | custom-call | tf_op jit(solution)/shard_map/halo/pallas_call | solution.py:80
  161.0 5.0 %gather_members.5 = f32[4,16,128]{2,1,0:T(8,128)} custom-call(f32[1,16,128]{2,1,0:T(8,128)} %bitcast.197), custom_call_target="tpu_custom_call" | custom-call | tf_op jit(solution)/shard_map/gather_members/pallas_call | solution.py:134
  (109 shorter events, 18.9 us)
Async XLA Ops:
  19.7 15.8 %copy-start.3 = (f32[6,136,128]{2,1,0:T(8,128)}, f32[6,136,128]{2,1,0:T(8,128)S(1)}, u32[]{:S(2)}) copy-start(f32[6,136,128]{2,1,0:T(8,128)S(1)} %get-tuple-element.50) | copy-start | bytes 1253380
  35.3 1.3 copy-start.19
  35.3 10.2 %copy-start = (f32[4,512,128]{2,1,0:T(8,128)S(1)}, f32[4,512,128]{2,1,0:T(8,128)}, u32[]{:S(2)}) copy-start(f32[4,512,128]{2,1,0:T(8,128)} %gather_members.4) | copy-start | bytes 3145732
  35.6 11.6 %copy-start.18 = (f32[128]{0:T(128)S(1)}, f32[128]{0:T(128)}, u32[]{:S(2)}) copy-start(f32[128]{0:T(128)} %param.12) | copy-start | bytes 1540
  35.6 11.6 %copy-start.20 = (f32[128]{0:T(128)S(1)}, f32[128]{0:T(128)}, u32[]{:S(2)}) copy-start(f32[128]{0:T(128)} %param.11) | copy-start | bytes 1540
  35.7 14.3 %copy-start.6 = (f32[4,128,127]{2,1,0:T(8,128)}, f32[4,128,127]{2,1,0:T(8,128)S(1)}, u32[]{:S(2)}) copy-start(f32[4,128,127]{2,1,0:T(8,128)S(1)} %get-tuple-element.47) | copy-start | bytes 780292
  35.7 14.3 %copy-start.8 = (f32[4,128,127]{2,1,0:T(8,128)}, f32[4,128,127]{2,1,0:T(8,128)S(1)}, u32[]{:S(2)}) copy-start(f32[4,128,127]{2,1,0:T(8,128)S(1)} %get-tuple-element.48) | copy-start | bytes 780292
  99.2 2.3 %copy-start.21 = (f32[512,512]{1,0:T(8,128)}, f32[512,512]{1,0:T(8,128)S(1)}, u32[]{:S(2)}) copy-start(f32[512,512]{1,0:T(8,128)S(1)} %fusion.41) | copy-start | bytes 3145732
  116.4 9.1 %copy-start.1 = (f32[512,512]{0,1:T(8,128)S(1)}, f32[512,512]{0,1:T(8,128)}, u32[]{:S(2)}) copy-start(f32[512,512]{0,1:T(8,128)} %get-tuple-element.71) | copy-start | bytes 3145732
  116.4 9.1 %copy-start.2 = (f32[512,512]{1,0:T(8,128)S(1)}, f32[512,512]{1,0:T(8,128)}, u32[]{:S(2)}) copy-start(f32[512,512]{1,0:T(8,128)} %copy.41) | copy-start | bytes 3145732
  125.5 3.5 %copy-start.22 = (f32[512,512]{1,0:T(8,128)S(1)}, f32[512,512]{1,0:T(8,128)}, u32[]{:S(2)}) copy-start(f32[512,512]{1,0:T(8,128)} %copy-done.21) | copy-start | bytes 3145732
  142.6 2.7 %copy-start.5 = (f32[512,128]{1,0:T(8,128)S(1)}, f32[512,128]{1,0:T(8,128)}, u32[]{:S(2)}) copy-start(f32[512,128]{1,0:T(8,128)} %get-tuple-element.10) | copy-start | bytes 786436
  143.2 3.0 %copy-start.16 = (f32[128,128]{1,0:T(8,128)S(1)}, f32[128,128]{1,0:T(8,128)}, u32[]{:S(2)}) copy-start(f32[128,128]{1,0:T(8,128)} %fusion.51) | copy-start | bytes 196612
  143.2 3.0 %copy-start.17 = (pred[4,128,128]{2,1,0:T(32,128)(4,1)S(1)}, pred[4,128,128]{2,1,0:T(32,128)(4,1)}, u32[]{:S(2)}) copy-start(pred[4,128,128]{2,1,0:T(32,128)(4,1)} %broadcast_compare_fusion) | copy-start | bytes 196612
  143.3 3.2 %copy-start.15 = (f32[128,128]{1,0:T(8,128)S(1)}, f32[128,128]{1,0:T(8,128)}, u32[]{:S(2)}) copy-start(f32[128,128]{1,0:T(8,128)} %fusion.53) | copy-start | bytes 196612
  143.3 3.4 %copy-start.13 = (f32[128,128]{1,0:T(8,128)S(1)}, f32[128,128]{1,0:T(8,128)}, u32[]{:S(2)}) copy-start(f32[128,128]{1,0:T(8,128)} %fusion.55) | copy-start | bytes 196612
  143.3 3.5 %copy-start.14 = (f32[128,128]{1,0:T(8,128)S(1)}, f32[128,128]{1,0:T(8,128)}, u32[]{:S(2)}) copy-start(f32[128,128]{1,0:T(8,128)} %fusion.57) | copy-start | bytes 196612
  143.3 3.7 %copy-start.7 = (f32[4,128,127]{2,1,0:T(8,128)S(1)}, f32[4,128,127]{2,1,0:T(8,128)}, u32[]{:S(2)}) copy-start(f32[4,128,127]{2,1,0:T(8,128)} %copy-done.6) | copy-start | bytes 780292
  143.3 3.7 %copy-start.9 = (f32[4,128,127]{2,1,0:T(8,128)S(1)}, f32[4,128,127]{2,1,0:T(8,128)}, u32[]{:S(2)}) copy-start(f32[4,128,127]{2,1,0:T(8,128)} %copy-done.8) | copy-start | bytes 780292
  158.9 1.0 copy-start.4
  158.9 1.1 copy-start.10
  158.9 1.1 copy-start.11
  158.9 1.2 copy-start.12

commit v2 on v1

--- a/solution.py
+++ b/solution.py
@@ -32,7 +32,7 @@
     return pltpu.CompilerParams(collective_id=ident, has_side_effects=True)
 
 
-def halo_body(n_space, last, first, low, high, send, recv):
+def halo_body(n_space, last, first, low, high, send, recv, others):
     s, m = lax.axis_index("space"), lax.axis_index("mem")
     barrier = pltpu.get_barrier_semaphore()
     has_low, has_high = s > 0, s < n_space - 1
@@ -45,7 +45,11 @@
     def _():
         pl.semaphore_signal(barrier, inc=1, device_id=(s + 1, m), device_id_type=MESH)
 
-    pl.semaphore_wait(barrier, has_low.astype(jnp.int32) + has_high.astype(jnp.int32))
+    for peer in others:
+        pl.semaphore_signal(barrier, inc=1, device_id=peer, device_id_type=MESH)
+    pl.semaphore_wait(
+        barrier, has_low.astype(jnp.int32) + has_high.astype(jnp.int32) + len(others)
+    )
 
     up = remote(last, low, send.at[0], recv.at[0], s + 1, m)
     down = remote(first, high, send.at[1], recv.at[1], s - 1, m)
@@ -72,9 +76,14 @@
     return finish
 
 
+def masked(n_space, low, high):
+    s = lax.axis_index("space")
+    return jnp.where(s > 0, low, 0.0), jnp.where(s < n_space - 1, high, 0.0)
+
+
 def halo(n_space, last, first, ident):
     def body(last_ref, first_ref, low, high, send, recv):
-        halo_body(n_space, last_ref, first_ref, low, high, send, recv)()
+        halo_body(n_space, last_ref, first_ref, low, high, send, recv, [])()
 
     shape = jax.ShapeDtypeStruct(last.shape, last.dtype)
     low, high = pl.pallas_call(
@@ -86,8 +95,67 @@
         compiler_params=params(ident),
         name="halo",
     )(last, first)
-    s = lax.axis_index("space")
-    return jnp.where(s > 0, low, 0.0), jnp.where(s < n_space - 1, high, 0.0)
+    return masked(n_space, low, high)
+
+
+def halo_gather(n_space, n_mem, last, first, block, ident):
+    half = 2 if n_mem % 2 == 0 else 1
+    wide = n_mem // half
+    members = block.shape[1]
+
+    def body(last_ref, first_ref, x, low, high, out, send, recv, own, p_send, p_recv, q_send, q_recv):
+        s, m = lax.axis_index("space"), lax.axis_index("mem")
+        p, q = m // half, lax.rem(m, half)
+        across = [lax.rem(p + k, wide) * half + q for k in range(1, wide)]
+        beside = [p * half + lax.rem(q + k, half) for k in range(1, half)]
+
+        def part(which):
+            return out.at[:, pl.ds(pl.multiple_of(which * members, members), members)]
+
+        mine = pltpu.make_async_copy(x, part(m), own.at[0])
+        mine.start()
+        finish = halo_body(
+            n_space, last_ref, first_ref, low, high, send, recv, [(s, to) for to in across + beside]
+        )
+        copies = []
+        for k, to in enumerate(across):
+            copies.append(remote(x, part(m), p_send.at[k], p_recv.at[k], s, to))
+            copies[-1].start()
+        hops = list(copies)
+        for k, to in enumerate(beside):
+            copies.append(remote(x, part(m), q_send.at[k, 0], q_recv.at[k, 0], s, to))
+            copies[-1].start()
+        for kp, hop in enumerate(hops):
+            from_p = lax.rem(p + wide - kp - 1, wide)
+            hop.wait_recv()
+            piece = part(from_p * half + q)
+            for k, to in enumerate(beside):
+                copies.append(remote(piece, piece, q_send.at[k, kp + 1], q_recv.at[k, kp + 1], s, to))
+                copies[-1].start()
+        finish()
+        mine.wait()
+        for copy in copies[len(hops) :]:
+            copy.wait_recv()
+        for copy in copies:
+            copy.wait_send()
+
+    shape = jax.ShapeDtypeStruct(last.shape, last.dtype)
+    full = list(block.shape)
+    full[1] *= n_mem
+    dma = pltpu.SemaphoreType.DMA
+    low, high, out = pl.pallas_call(
+        body,
+        out_shape=(shape, shape, jax.ShapeDtypeStruct(tuple(full), block.dtype)),
+        in_specs=[VMEM_SPEC] * 3,
+        out_specs=(VMEM_SPEC,) * 3,
+        scratch_shapes=[
+            dma((2,)), dma((2,)), dma((1,)), dma((wide,)), dma((wide,)),
+            dma((half, wide)), dma((half, wide)),
+        ],
+        compiler_params=params(ident),
+        name="halo_gather",
+    )(last, first, block)
+    return *masked(n_space, low, high), out
 
 
 def gather_members(n_mem, arrays, dims, ident):
@@ -180,14 +248,14 @@
         total = buf[0]
         for k in range(1, n_space):
             total = total + buf[k]
-        out[m, b, a] = total
+        out[m, a, b] = total
 
         waits = list(scatter)
         stage_a = []
         for k in range(1, far):
             to = lax.rem(a + k, far)
             copy = remote(
-                out.at[m, b, a], out.at[m, b, a], a_send.at[k], a_recv.at[k], to * near + b, m
+                out.at[m, a, b], out.at[m, a, b], a_send.at[k], a_recv.at[k], to * near + b, m
             )
             copy.start()
             stage_a.append(copy)
@@ -211,7 +279,7 @@
                 pend.append((start, index, kb))
             for start_, index_, kb in pend:
                 from_b = lax.rem(b + near - kb, near)
-                piece = out.at[m, from_b, pl.ds(start_, group)]
+                piece = out.at[m, pl.ds(start_, group), from_b]
                 remote(piece, piece, b_send.at[kb, index_], b_recv.at[kb, index_], s, m).wait_recv()
                 flow(
                     out, s, m, from_b, p, q, start_, index_, kb, group, near, half, wide,
@@ -222,7 +290,7 @@
                 which_b = lax.rem(b + near - kb, near)
                 for kp in range(1, wide):
                     from_p = lax.rem(p + wide - kp, wide)
-                    piece = out.at[from_p * half + q, which_b, pl.ds(start, group)]
+                    piece = out.at[from_p * half + q, pl.ds(start, group), which_b]
                     remote(
                         piece, piece, p_send.at[kp, kb, index], p_recv.at[kp, kb, index], s, m
                     ).wait_recv()
@@ -241,7 +309,7 @@
                     from_p = lax.rem(p + wide - kp, wide)
                     for kq in range(1, half):
                         from_q = lax.rem(q + half - kq, half)
-                        piece = out.at[from_p * half + from_q, which_b, pl.ds(start, group)]
+                        piece = out.at[from_p * half + from_q, pl.ds(start, group), which_b]
                         remote(
                             piece, piece, q_send.at[kq, kp, kb, index],
                             q_recv.at[kq, kp, kb, index], s, m,
@@ -253,7 +321,7 @@
         out, s, m, which_b, p, q, start, index, kb, group, near, half, wide,
         b_send, b_recv, p_send, p_recv, q_send, q_recv, waits,
     ):
-        piece = out.at[m, which_b, pl.ds(start, group)]
+        piece = out.at[m, pl.ds(start, group), which_b]
         for kp in range(1, wide):
             copy = remote(
                 piece, piece, p_send.at[kp, kb, index], p_recv.at[kp, kb, index],
@@ -278,7 +346,7 @@
     dma = pltpu.SemaphoreType.DMA
     out = pl.pallas_call(
         body,
-        out_shape=jax.ShapeDtypeStruct((n_mem, near, far, height, width), rows.dtype),
+        out_shape=jax.ShapeDtypeStruct((n_mem, far, near, height, width), rows.dtype),
         in_specs=[VMEM_SPEC],
         out_specs=VMEM_SPEC,
         scratch_shapes=[
@@ -295,6 +363,108 @@
     return out
 
 
+def split(x):
+    lead = x.astype(jnp.bfloat16)
+    return lead, (x - lead.astype(jnp.float32)).astype(jnp.bfloat16)
+
+
+def mm3(a, b):
+    plain = lambda x, y: jnp.dot(x, y, preferred_element_type=jnp.float32)
+    return plain(a[0], b[0]) + (plain(a[0], b[1]) + plain(a[1], b[0]))
+
+
+def analyse(done, cot_full, anom_full, innovation, precision, tanh_picked, onehot, sea, members):
+    total = done.shape[0]
+    rows, _, cols = cot_full.shape
+
+    def body(done, cot, anom, innov, prec, tanh, hot, sea, out, f_ref, f2_ref, t_ref, s_ref, u_ref, y_ref, v_ref):
+        scale = jnp.sqrt(jnp.float32(total - 1))
+        offset = pl.multiple_of(lax.axis_index("mem") * members, members)
+        mine = pl.ds(offset, members)
+        diagonal = lax.broadcasted_iota(jnp.int32, (total, total), 0) == lax.broadcasted_iota(
+            jnp.int32, (total, total), 1
+        )
+        identity = diagonal.astype(jnp.float32)
+        whole = lambda x: jnp.sum(jnp.sum(x, axis=0, keepdims=True), axis=1, keepdims=True)
+        system = identity + done[:, :total]
+        norm = jnp.sqrt(whole(system * system))
+        root = jnp.sqrt(norm)
+        f_ref[...] = 1.5 * identity - 0.5 * (system / norm)
+        f_split = split(f_ref[...])
+        f2_ref[...] = mm3(f_split, f_split)
+        f2_split = split(f2_ref[...])
+        t_ref[...] = (
+            1.5 * f_ref[...] + mm3(f2_split, split(f2_ref[...] - 1.5 * f_ref[...]))
+        ) / root
+        t_split = split(t_ref[...])
+        pull = done[:, 2 * total :]
+        mean_bar = jnp.sum(done[:, total : 2 * total], axis=1, keepdims=True)
+        first = mm3(t_split, split(jnp.concatenate([pull, jnp.broadcast_to(mean_bar, pull.shape)], axis=1)))
+        v_ref[...] = mm3(t_split, split(first))
+        width = pull.shape[1]
+        row = lambda x: x.T[:1]
+        s_ref[...] = (
+            scale * done[:, total : 2 * total]
+            + mean_bar * row(first[:, :width])
+            + first[:, width : width + 1] * row(pull)
+        )
+        weight = 0.5 * (s_ref[...] + s_ref[...].T)
+        scale_bar = -0.5 * whole(weight * t_ref[...]) / norm
+        s_ref[...] = weight / root
+        s_split = split(s_ref[...])
+        u_ref[...] = mm3(s_split, f2_split)
+        y_ref[...] = mm3(s_split, split(2.0 * f2_ref[...] - 1.5 * f_ref[...]))
+        y_ref[...] = 0.5 * (y_ref[...] + y_ref[...].T)
+        approach = 1.5 * s_ref[...] - 1.5 * u_ref[...]
+        approach = whole(
+            approach * (3.0 * identity - 2.0 * f_ref[...])
+            + 2.0 * y_ref[...] * (3.0 * f_ref[...] - 2.0 * f2_ref[...])
+        )
+        scale_bar = scale_bar + 0.5 * approach / norm
+
+        centred = lambda ref: ref[mine, :] - jnp.sum(ref[...], axis=0, keepdims=True) / total
+        f_mine = centred(f_ref)
+        bar = 1.5 * centred(s_ref) - 0.75 * (centred(u_ref) + mm3(split(centred(f2_ref)), s_split))
+        bar = bar + mm3(split(centred(y_ref)), f_split) + mm3(split(f_mine), split(y_ref[...]))
+        unit = (
+            lax.broadcasted_iota(jnp.int32, (members, total), 0) + offset
+            == lax.broadcasted_iota(jnp.int32, (members, total), 1)
+        ).astype(jnp.float32) - 1.0 / total
+        system_mine = norm * (3.0 * unit - 2.0 * f_mine)
+        sym = 2.0 * (-0.5 * bar + scale_bar * system_mine) / norm
+        pull_bar = v_ref[:, width:]
+        sym = sym - (scale / total) * row(pull_bar)
+        pull_mine = v_ref[mine, width:][:, :1] - jnp.sum(pull_bar[:, :1], axis=0, keepdims=True) / total
+        mean_weights = v_ref[:, :1]
+        mix = t_ref[mine, :] + v_ref[mine, :width][:, :1] / scale
+        row_weights = (
+            jnp.sum(t_ref[...], axis=0, keepdims=True)
+            + jnp.sum(mean_weights, axis=0, keepdims=True) / scale
+        )
+        mix = mix + (1.0 - row_weights) / total
+        observed = (prec[...] / scale) * (mm3(split(sym), split(anom[...])) + pull_mine * innov[...])
+        picked = observed * (1.0 + 0.5 * (1.0 - tanh[...] * tanh[...]))
+        mix_split, picked_split = split(mix), split(picked)
+        for r in range(rows):
+            mark = hot[r].astype(jnp.bfloat16)
+            spread = jnp.dot(picked_split[0], mark, preferred_element_type=jnp.float32) + jnp.dot(
+                picked_split[1], mark, preferred_element_type=jnp.float32
+            )
+            out[r] = sea[r] * (mm3(mix_split, split(cot[r])) + spread)
+
+    square = pltpu.VMEM((total, total), jnp.float32)
+    return pl.pallas_call(
+        body,
+        out_shape=jax.ShapeDtypeStruct((rows, members, cols), jnp.float32),
+        in_specs=[VMEM_SPEC] * 8,
+        out_specs=VMEM_SPEC,
+        scratch_shapes=[square] * 6 + [pltpu.VMEM((total, 2 * (done.shape[1] - 2 * total)), jnp.float32)],
+        compiler_params=pltpu.CompilerParams(vmem_limit_bytes=60 * 1024 * 1024),
+        cost_estimate=pl.CostEstimate(flops=10 * total**3, bytes_accessed=8 * total**2, transcendentals=0),
+        name="analyse",
+    )(done, cot_full, anom_full, innovation, precision, tanh_picked, onehot, sea)
+
+
 def neighbours(ext):
     center, north, south = ext[1:-1], ext[:-2], ext[2:]
     border = jnp.zeros_like(center[..., :1])
@@ -349,8 +519,7 @@
         axis=1,
     )
     packed = jnp.concatenate([prior_t, aux], axis=1)
-    low, high = halo(n_space, packed[-2:], packed[:2], 1)
-    (cot_full,) = gather_members(n_mem, [cot_t], [1], 2)
+    low, high, cot_full = halo_gather(n_space, n_mem, packed[-2:], packed[:2], cot_t, 1)
     ext = jnp.concatenate([low, packed, high], axis=0)
     prior_ext = ext[:, :members]
     coef_ext = jnp.transpose(ext[:, members : members + 4], (1, 0, 2))[:, :, None]
@@ -377,56 +546,13 @@
     block = jnp.concatenate(
         [gram_rows, cross_rows, jnp.broadcast_to(pull_rows[:, None], (members, 128))], axis=1
     )
-    near = 2 if n_space % 2 == 0 else 1
     block = block.reshape(n_space, members // n_space, -1)
     done = reduce_gather(n_space, n_mem, block, 4)
-    done = jnp.transpose(done, (0, 2, 1, 3, 4)).reshape(total, -1)
-    gram, cross, pull = done[:, :total], done[:, total : 2 * total], done[:, 2 * total]
-
-    identity = jnp.eye(total, dtype=jnp.float32)
-    system = identity + gram
-    norm = jnp.sqrt(jnp.sum(system * system))
-    root = jnp.sqrt(norm)
-    approach = system / norm
-    factor = 1.5 * identity - 0.5 * approach
-    square = mm(factor, factor)
-    transform = (1.5 * factor + mm(square, square - 1.5 * factor)) / root
-    mid_pull = jnp.sum(transform * pull[None, :], axis=1)
-    mean_weights = jnp.sum(transform * mid_pull[None, :], axis=1)
-    mean_bar = jnp.sum(cross, axis=1)
-    mid_bar = jnp.sum(transform * mean_bar[None, :], axis=1)
-    pull_bar = jnp.sum(transform * mid_bar[None, :], axis=1)
-    half_weight = (
-        scale * cross + mean_bar[:, None] * mid_pull[None, :] + mid_bar[:, None] * pull[None, :]
-    )
-    weight_bar = 0.5 * (half_weight + half_weight.T)
-    polar_bar = weight_bar / root
-    scale_bar = -0.5 * jnp.sum(weight_bar * transform) / norm
-    bar_square = mm(polar_bar, square)
-    bar_mixed = mm(polar_bar, 2.0 * square - 1.5 * factor)
-    square_bar = 0.5 * (bar_mixed + bar_mixed.T)
-    bar_factor = mm(square_bar, factor)
-    half_bar = 0.75 * polar_bar - 1.5 * 0.5 * bar_square + bar_factor
-    approach_bar = -0.5 * (half_bar + half_bar.T)
-    scale_bar = scale_bar - jnp.sum(approach_bar * approach) / norm
-    sym_bar = 2.0 * (approach_bar + scale_bar * system) / norm
-
-    offset = m * members
-    take = lambda x: lax.dynamic_slice_in_dim(x, offset, members, 0)
-    mix_rows = take(transform) + take(mean_weights)[:, None] / scale
-    row_weights = jnp.sum(transform, axis=0) + jnp.sum(mean_weights) / scale
-    mix_rows = mix_rows + ((1.0 - row_weights) / total)[None, :]
-    sym_rows = take(sym_bar) - (jnp.sum(sym_bar, axis=0) / total)[None, :]
-    sym_rows = sym_rows - (scale / total * pull_bar)[None, :]
-    observed_bar = (precision / scale) * (
-        mm(sym_rows, anom_full)
-        + (take(pull_bar) - jnp.sum(pull_bar) / total)[:, None] * innovation[None, :]
-    )
-    picked_bar = observed_bar * (1.0 + 0.5 * (1.0 - tanh_picked * tanh_picked))
-    field_bar = jnp.stack(
-        [mm(mix_rows, cot_full[r]) + mm(picked_bar, onehot[r]) for r in range(rows)]
-    )
-    second_bar = sea_ext[2:-2] * field_bar
+    done = done.reshape(total, -1)
+    second_bar = analyse(
+        done, cot_full, anom_full, innovation[None], precision[None], tanh_picked,
+        onehot, sea_ext[2:-2], members,
+    )
     low_bar, high_bar = halo(n_space, second_bar[-2:], second_bar[:2], 5)
     bar_ext = jnp.concatenate([low_bar, second_bar, high_bar], axis=0)
     first_bar = sea_ext[1:-1] * transpose_step(bar_ext, coef_ext)

time: 170 us -> 117 us (0.69)
  matrix products: 25.3 us -> 3.6 us
  local copies, waits for them, and re-layouts: 23.2 us -> 8.29 us
  other arithmetic: 26.1 us -> 14.4 us
  between operations: 4.55 us -> 0.96 us
    pallas_call x1 -> x3, Pallas kernels: 41 us -> 65.4 us  [the longest x1 40.8 us: reduce_gather(): pl.pallas_call(body, out_shape=jax.ShapeDtypeStruct((n_mem, far, near, he...]
    dot_general x17 -> x3, matrix products: 25.3 us -> 3.6 us  [dot(): lax.dot_general(a, b, ((a_dims, b_dims), ((), ())), precision=precision,...]
    pallas_call x3 -> x2, Pallas kernels: 27.6 us -> 11.8 us  [gather_members(): pl.pallas_call(body, out_shape=tuple(shapes), in_specs=[VMEM_SPEC] * coun...]
    reduce_sum x7 -> x0, other arithmetic: 14 us -> none  [the longest x1 3.49 us: local(): mean_weights = jnp.sum(transform * mid_pull[None, :], axis=1)]
    pallas_call x2 -> x1, Pallas kernels: 20.6 us -> 11.5 us  [halo(): pl.pallas_call(body, out_shape=(shape, shape), in_specs=[VMEM_SPEC] * 2,...]
    add x2 -> x0, local copies, waits for them, and re-layouts: 5.06 us -> none  [the longest x1 2.53 us: local(): half_bar = 0.75 * polar_bar - 1.5 * 0.5 * bar_square + bar_factor]
    unnamed x58 -> x25, local copies, waits for them, and re-layouts: 7.49 us -> 4.6 us
    div x1 -> x0, local copies, waits for them, and re-layouts: 2.55 us -> none  [local(): transform = (1.5 * factor + mm(square, square - 1.5 * factor)) / root]
where the time goes in v2:
time: 117 us; the launch traced here: 116 us
  Pallas kernels  88.7 us (76%)
  other arithmetic  14.4 us (12%)
  local copies, waits for them, and re-layouts  8.29 us (7%)
  matrix products  3.6 us (3%)
    pallas_call x1, Pallas kernels, reduce_gather(): pl.pallas_call(body, out_shape=jax.ShapeDtypeStruct((n_mem, far, near, he...  40.8 us
    pallas_call x1, Pallas kernels, halo_gather(): pl.pallas_call(body, out_shape=(shape, shape, jax.ShapeDtypeStruct(tuple(...  14 us
    pallas_call x2, Pallas kernels, gather_members(): pl.pallas_call(body, out_shape=tuple(shapes), in_specs=[VMEM_SPEC] * coun...  11.8 us
    pallas_call x1, Pallas kernels, halo(): pl.pallas_call(body, out_shape=(shape, shape), in_specs=[VMEM_SPEC] * 2,...  11.5 us
    pallas_call x1, Pallas kernels, analyse(): pl.pallas_call(body, out_shape=jax.ShapeDtypeStruct((rows, members, cols)...  10.5 us
    unnamed x25, local copies, waits for them, and re-layouts  4.6 us
    dot_general x3, matrix products, dot(): lax.dot_general(a, b, ((a_dims, b_dims), ((), ())), precision=precision,...  3.6 us

profile of v2, /device:TPU:0, one launch (start us, length us, event | category | flops | bytes accessed | tf_op | source)
XLA Modules:
  0.0 115.9 jit_solution(10615295435846286304)
XLA Ops:
  0.6 0.7 convert_element_type.6
  1.3 1.0 copy.61
  2.3 0.7 copy.62
  3.0 0.7 fusion.38
  3.7 1.7 %copy.60 = f32[128,4,128]{2,0,1:T(8,128)} copy(f32[128,4,128]{2,1,0:T(4,128)} %param.13) | data formatting | bytes 524288 | tf_op args[6]
  5.4 14.0 %halo_gather.1 = (f32[2,136,128]{2,1,0:T(8,128)}, f32[2,136,128]{2,1,0:T(8,128)}, f32[4,512,128]{2,1,0:T(8,128)}) custom-call(f32[2,136,128]{2,1,0:T(8,128)} %get-tuple-element.40.last_ref, f32[2,136,128]{2,1,0:T(8,128)} %get-tuple-element.39.first_ref, f32[4,128,128]{2,1,0:T(8,128)} %bitcast.100), custom_call_target="tpu_custom_call" | custom-call | tf_op jit(solution)/shard_map/halo_gather/pallas_call | solution.py:146
  19.4 0.9 broadcast_select_fusion
  21.5 1.0 multiply_add_fusion
  22.5 0.6 pad_bitcast_fusion.refs_1_
  23.1 6.8 %gather_members.2 = (f32[512,128]{1,0:T(8,128)}, f32[4,8,128]{2,1,0:T(8,128)}) custom-call(f32[128,128]{1,0:T(8,128)} %get-tuple-element.62.refs_0_, f32[1,8,128]{2,1,0:T(8,128)} %pad_bitcast_fusion.refs_1_), custom_call_target="tpu_custom_call" | custom-call | tf_op jit(solution)/shard_map/gather_members/pallas_call | solution.py:202
  29.8 1.0 reduce_sum.118
  30.9 0.5 broadcast_multiply_fusion.1
  31.4 1.7 %multiply_multiply_fusion.anom = f32[512,128]{1,0:T(8,128)} fusion(f32[512,128]{1,0:T(8,128)} %get-tuple-element.11, f32[128]{0:T(128)S(1)} %copy-done.4, f32[128]{0:T(128)S(1)} %get-tuple-element.61), kind=kLoop, calls=%fused_computation.56 | loop fusion | flops 196608 | bytes 525312 | tf_op jit(solution)/shard_map/div | solution.py:540
  33.1 1.9 %fusion.28 = f32[128,512]{1,0:T(8,128)} fusion(f32[128]{0:T(128)S(1)} %copy-done.4, f32[128]{0:T(128)S(1)} %get-tuple-element.61, f32[128,128]{1,0:T(8,128)S(1)} %get-tuple-element.63, f32[512,128]{1,0:T(8,128)} %get-tuple-element.11), kind=kOutput, calls=%fused_computation.69 | convolution fusion | flops 50610176 | bytes 590848 | tf_op jit(solution)/shard_map/dot_general | solution.py:16
  35.0 0.7 reduce_sum.119
  35.8 0.7 convolution_bitcast_fusion
  36.4 0.6 fusion.41
  37.1 1.8 %pad_maximum_fusion = f32[128,1152]{1,0:T(8,128)} fusion(f32[128,128]{1,0:T(8,128)S(1)} %broadcast_in_dim.46, f32[128,512]{1,0:T(8,128)S(1)} %convolution_bitcast_fusion, f32[128,512]{1,0:T(8,128)} %fusion.28), kind=kLoop, calls=%fused_computation.2 | loop fusion | flops 294912 | bytes 1179648 | tf_op jit(solution)/shard_map/concatenate | solution.py:546
  39.0 40.8 %reduce_gather.1 = f32[4,4,2,16,1152]{4,3,2,1,0:T(8,128)} custom-call(f32[8,16,1152]{2,1,0:T(8,128)} %bitcast.99), custom_call_target="tpu_custom_call" | custom-call | tf_op jit(solution)/shard_map/reduce_gather/pallas_call | solution.py:347
  79.8 0.8 compare_convert_fusion.hot
  80.6 10.5 %analyse.1 = f32[4,128,128]{2,1,0:T(8,128)} custom-call(f32[512,1152]{1,0:T(8,128)} %bitcast.98, f32[4,512,128]{2,1,0:T(8,128)} %get-tuple-element.13.cot, f32[512,128]{1,0:T(8,128)} %multiply_multiply_fusion.anom, f32[1,128]{1,0:T(1,128)} %bitcast.147, f32[1,128]{1,0:T(1,128)} %bitcast.133, f32[128,128]{1,0:T(8,128)} %get-tuple-element.47.tanh, ...), custom_call_target="tpu_custom_call" | custom-call | flops 1342177280 | bytes 2097152 | tf_op jit(solution)/shard_map/analyse/pallas_call | solution.py:456
  91.1 1.2 %multiply_reduce_fusion.5 = (f32[4,128]{1,0:T(4,128)S(1)}, f32[4,128]{1,0:T(4,128)S(1)}, f32[4,128]{1,0:T(4,128)S(1)}, f32[4,128]{1,0:T(4,128)S(1)}) fusion(f32[4,128,128]{2,1,0:T(8,128)} %analyse.1, f32[6,128,128]{2,1,0:T(8,128)S(1)} %fusion.4, f32[4,128,127]{2,1,0:T(8,128)S(1)} %get-tuple-element.35, f32[4,128,127]{2,1,0:T(8,128)S(1)} %get-tuple-element.36), kind=kLoop, calls=%fused_computation.53 | loop fusion | flops 784384 | bytes 1576960 | tf_op jit(solution)/shard_map/reduce_sum | solution.py:502
  92.3 1.7 %fusion.40 = (f32[2,128,128]{2,1,0:T(8,128)}, f32[2,128,128]{2,1,0:T(8,128)}) fusion(f32[4,128,128]{2,1,0:T(8,128)} %analyse.1), kind=kLoop, calls=%fused_computation.103 | loop fusion | bytes 524288 | tf_op jit(solution)/shard_map/slice | solution.py:556
  94.0 11.5 %halo.1 = (f32[2,128,128]{2,1,0:T(8,128)}, f32[2,128,128]{2,1,0:T(8,128)}) custom-call(f32[2,128,128]{2,1,0:T(8,128)} %get-tuple-element.46.last_ref, f32[2,128,128]{2,1,0:T(8,128)} %get-tuple-element.45.first_ref), custom_call_target="tpu_custom_call" | custom-call | tf_op jit(solution)/shard_map/halo/pallas_call | solution.py:89
  105.5 0.9 broadcast_select_fusion.2
  107.4 0.3 copy-done.1
  107.7 0.3 fusion.16
  108.0 0.6 maximum_add_fusion
  108.6 5.0 %gather_members.3 = f32[4,16,128]{2,1,0:T(8,128)} custom-call(f32[1,16,128]{2,1,0:T(8,128)} %bitcast.124), custom_call_target="tpu_custom_call" | custom-call | tf_op jit(solution)/shard_map/gather_members/pallas_call | solution.py:202
  113.6 0.8 reduce_sum.129
  114.4 0.6 broadcast_multiply_fusion
  115.0 0.9 copy.20
  (46 shorter events, 1.9 us)
Async XLA Ops:
  1.3 19.9 %copy-start.3 = (f32[4,128]{1,0:T(4,128)}, f32[4,128]{1,0:T(4,128)S(1)}, u32[]{:S(2)}) copy-start(f32[4,128]{1,0:T(4,128)S(1)} %convert_element_type.6) | copy-start | bytes 6148
  20.8 0.7 copy-start.5
  20.8 10.1 %copy-start.4 = (f32[128]{0:T(128)S(1)}, f32[128]{0:T(128)}, u32[]{:S(2)}) copy-start(f32[128]{0:T(128)} %param.12) | copy-start | bytes 1540
  20.8 10.1 %copy-start.6 = (f32[128]{0:T(128)S(1)}, f32[128]{0:T(128)}, u32[]{:S(2)}) copy-start(f32[128]{0:T(128)} %param.11) | copy-start | bytes 1540
  21.1 14.7 %copy-start.2 = (f32[4,512,128]{2,1,0:T(8,128)S(1)}, f32[4,512,128]{2,1,0:T(8,128)}, u32[]{:S(2)}) copy-start(f32[4,512,128]{2,1,0:T(8,128)} %get-tuple-element.13.cot) | copy-start | bytes 3145732
  91.1 15.4 %copy-start = (f32[4,128,128]{2,1,0:T(8,128)S(1)}, f32[4,128,128]{2,1,0:T(8,128)}, u32[]{:S(2)}) copy-start(f32[4,128,128]{2,1,0:T(8,128)} %analyse.1) | copy-start | bytes 786436
  106.8 1.0 copy-start.1

commit v3 on v2

--- a/solution.py
+++ b/solution.py
@@ -76,11 +76,6 @@
     return finish
 
 
-def masked(n_space, low, high):
-    s = lax.axis_index("space")
-    return jnp.where(s > 0, low, 0.0), jnp.where(s < n_space - 1, high, 0.0)
-
-
 def halo(n_space, last, first, ident):
     def body(last_ref, first_ref, low, high, send, recv):
         halo_body(n_space, last_ref, first_ref, low, high, send, recv, [])()
@@ -95,7 +90,7 @@
         compiler_params=params(ident),
         name="halo",
     )(last, first)
-    return masked(n_space, low, high)
+    return low, high
 
 
 def halo_gather(n_space, n_mem, last, first, block, ident):
@@ -155,7 +150,7 @@
         compiler_params=params(ident),
         name="halo_gather",
     )(last, first, block)
-    return *masked(n_space, low, high), out
+    return low, high, out
 
 
 def gather_members(n_mem, arrays, dims, ident):
@@ -386,7 +381,19 @@
         )
         identity = diagonal.astype(jnp.float32)
         whole = lambda x: jnp.sum(jnp.sum(x, axis=0, keepdims=True), axis=1, keepdims=True)
-        system = identity + done[:, :total]
+        for p in range(4):
+            here, there = pl.ds(p * members, members), pl.ds((p + 1) % 4 * members, members)
+            s_ref[here, here] = done[here, total : total + members]
+            edge = done[here, total + members : total + 2 * members]
+            s_ref[here, there] = edge
+            s_ref[there, here] = edge.T
+        for p in range(2):
+            here, there = pl.ds(p * members, members), pl.ds((p + 2) * members, members)
+            pair = slice(total + 2 * members, total + 2 * members + members // 2)
+            edge = jnp.concatenate([done[here, pair], done[there, pair]], axis=1)
+            s_ref[here, there] = edge
+            s_ref[there, here] = edge.T
+        system = identity + s_ref[...]
         norm = jnp.sqrt(whole(system * system))
         root = jnp.sqrt(norm)
         f_ref[...] = 1.5 * identity - 0.5 * (system / norm)
@@ -397,14 +404,14 @@
             1.5 * f_ref[...] + mm3(f2_split, split(f2_ref[...] - 1.5 * f_ref[...]))
         ) / root
         t_split = split(t_ref[...])
-        pull = done[:, 2 * total :]
-        mean_bar = jnp.sum(done[:, total : 2 * total], axis=1, keepdims=True)
+        pull = jnp.broadcast_to(done[:, total + 3 * members - 1 :], (total, 128))
+        mean_bar = jnp.sum(done[:, :total], axis=1, keepdims=True)
         first = mm3(t_split, split(jnp.concatenate([pull, jnp.broadcast_to(mean_bar, pull.shape)], axis=1)))
         v_ref[...] = mm3(t_split, split(first))
         width = pull.shape[1]
         row = lambda x: x.T[:1]
         s_ref[...] = (
-            scale * done[:, total : 2 * total]
+            scale * done[:, :total]
             + mean_bar * row(first[:, :width])
             + first[:, width : width + 1] * row(pull)
         )
@@ -458,107 +465,204 @@
         out_shape=jax.ShapeDtypeStruct((rows, members, cols), jnp.float32),
         in_specs=[VMEM_SPEC] * 8,
         out_specs=VMEM_SPEC,
-        scratch_shapes=[square] * 6 + [pltpu.VMEM((total, 2 * (done.shape[1] - 2 * total)), jnp.float32)],
+        scratch_shapes=[square] * 6 + [pltpu.VMEM((total, 256), jnp.float32)],
         compiler_params=pltpu.CompilerParams(vmem_limit_bytes=60 * 1024 * 1024),
         cost_estimate=pl.CostEstimate(flops=10 * total**3, bytes_accessed=8 * total**2, transcendentals=0),
         name="analyse",
     )(done, cot_full, anom_full, innovation, precision, tanh_picked, onehot, sea)
 
 
-def neighbours(ext):
-    center, north, south = ext[1:-1], ext[:-2], ext[2:]
-    border = jnp.zeros_like(center[..., :1])
-    west = jnp.concatenate([border, center[..., :-1]], axis=-1)
-    east = jnp.concatenate([center[..., 1:], border], axis=-1)
-    return center, north, south, west, east
-
-
-def substep(ext, coef, sea):
-    center, north, south, west, east = neighbours(ext)
-    return sea * (
-        center
-        + coef[0] * (north - center)
-        + coef[1] * (south - center)
-        + coef[2] * (west - center)
-        + coef[3] * (east - center)
-    )
-
-
-def transpose_step(ext, coef_ext):
-    center = ext[1:-1]
-    inner = coef_ext[:, 1:-1]
-    from_south = coef_ext[0, 2:] * ext[2:]
-    from_north = coef_ext[1, :-2] * ext[:-2]
-    border = jnp.zeros_like(center[..., :1])
-    from_east = jnp.concatenate([(inner[2] * center)[..., 1:], border], axis=-1)
-    from_west = jnp.concatenate([border, (inner[3] * center)[..., :-1]], axis=-1)
-    keeping = 1.0 - inner[0] - inner[1] - inner[2] - inner[3]
-    return center * keeping + from_south + from_north + from_east + from_west
-
-
-def coef_terms(weight, ext):
-    center, north, south, west, east = neighbours(ext)
-    return jnp.stack(
-        [jnp.sum(weight * (side - center), axis=1) for side in (north, south, west, east)]
-    )
+def side(x, step):
+    lane = lax.broadcasted_iota(jnp.int32, x.shape, 1)
+    last = x.shape[1] - 1
+    if step > 0:
+        return jnp.where(lane == 0, 0.0, pltpu.roll(x, 1, 1))
+    return jnp.where(lane == last, 0.0, pltpu.roll(x, last, 1))
+
+
+def chosen(n_space, low, packed, high, i, where):
+    s = lax.axis_index("space")
+    rows = packed.shape[0]
+    if i < 2:
+        return jnp.where(s > 0, low[i, where], 0.0)
+    if i < rows + 2:
+        return packed[i - 2, where]
+    return jnp.where(s < n_space - 1, high[i - rows - 2, where], 0.0)
+
+
+def forecast(n_space, low, packed, high, onehot, members):
+    rows, _, cols = packed.shape
+    sites = onehot.shape[1]
+
+    def body(low, packed, high, hot, first, state, observed, tanh, sums):
+        def row(i):
+            return chosen(n_space, low, packed, high, i, slice(0, members))
+
+        def aux(i, k):
+            return chosen(n_space, low, packed, high, i, slice(members + k, members + k + 1))
+
+        def step(center, north, south, i):
+            return aux(i, 4) * (
+                center
+                + aux(i, 0) * (north - center)
+                + aux(i, 1) * (south - center)
+                + aux(i, 2) * (side(center, 1) - center)
+                + aux(i, 3) * (side(center, -1) - center)
+            )
+
+        for i in range(1, rows + 3):
+            first[i - 1] = step(row(i), row(i - 1), row(i + 1), i)
+        picked = jnp.zeros((members, sites), jnp.float32)
+        sums[...] = jnp.zeros_like(sums)
+        for r in range(rows):
+            state[r] = step(first[r + 1], first[r], first[r + 2], r + 2)
+            sums[0, r : r + 1] = jnp.sum(state[r], axis=0, keepdims=True)
+            picked = picked + lax.dot_general(
+                state[r], hot[r], (((1,), (1,)), ((), ())), precision=HIGHEST,
+                preferred_element_type=jnp.float32,
+            )
+        tanh[...] = jnp.tanh(picked)
+        observed[...] = picked + 0.5 * tanh[...]
+
+    shape = lambda *dims: jax.ShapeDtypeStruct(dims, jnp.float32)
+    return pl.pallas_call(
+        body,
+        out_shape=(
+            shape(rows + 2, members, cols), shape(rows, members, cols), shape(members, sites),
+            shape(members, sites), shape(1, rows + -rows % 8, cols),
+        ),
+        in_specs=[VMEM_SPEC] * 4,
+        out_specs=(VMEM_SPEC,) * 5,
+        name="forecast",
+    )(low, packed, high, onehot)
+
+
+def prepare(n_mem, state, obs_full, sums, precision, data, cot_full):
+    rows, members, cols = state.shape
+    total, sites = obs_full.shape
+    assert n_mem == 4
+    middle = members // 2
+
+    def nt3(a, b):
+        plain = lambda x, y: lax.dot_general(
+            x, y, (((1,), (1,)), ((), ())), preferred_element_type=jnp.float32
+        )
+        return plain(a[0], b[0]) + (plain(a[0], b[1]) + plain(a[1], b[0]))
+
+    def body(state, obs, sums, prec, data, cot, block, anom, innov):
+        m = lax.axis_index("mem")
+        scale = jnp.sqrt(jnp.float32(total - 1))
+        average = jnp.sum(sums[...], axis=0) / total
+        mean = jnp.sum(obs[...], axis=0, keepdims=True) / total
+        anom[...] = (obs[...] - mean) * prec[...] / scale
+        innov[...] = prec[...] * (data[...] - mean)
+        cross = jnp.zeros((members, total), jnp.float32)
+        for r in range(rows):
+            deviation = (state[r] - average[r : r + 1]) / scale
+            cross = cross + nt3(split(deviation), split(cot[r]))
+        block[:, :total] = cross
+        at = lambda start, size: anom[pl.ds(pl.multiple_of(start, middle), size), :]
+        own = at(m * members, members)
+        own_split = split(own)
+        block[:, total : total + members] = nt3(own_split, own_split)
+        beside = at(lax.rem(m + 1, n_mem) * members, members)
+        block[:, total + members : total + 2 * members] = nt3(own_split, split(beside))
+        low, high = lax.rem(m, 2), m // 2
+        halves = nt3(
+            split(at(low * members, members)),
+            split(at((low + 2) * members + high * middle, middle)),
+        )
+        pull = jnp.sum(own * innov[...], axis=1, keepdims=True)
+        block[:, total + 2 * members :] = jnp.concatenate(
+            [halves, jnp.broadcast_to(pull, (members, middle))], axis=1
+        )
+
+    shape = lambda *dims: jax.ShapeDtypeStruct(dims, jnp.float32)
+    return pl.pallas_call(
+        body,
+        out_shape=(shape(members, total + 3 * members), shape(total, sites), shape(1, sites)),
+        in_specs=[VMEM_SPEC] * 6,
+        out_specs=(VMEM_SPEC,) * 3,
+        name="prepare",
+    )(state, obs_full, sums, precision, data, cot_full)
+
+
+def backward(n_space, low_bar, second_bar, high_bar, low, packed, high, first_ext):
+    rows, members, cols = second_bar.shape
+
+    def body(low_bar, second, high_bar, low, packed, high, first_ext, grad, coef, first_bar):
+        def bar(i):
+            return chosen(n_space, low_bar, second, high_bar, i, slice(0, members))
+
+        def prior(i):
+            return chosen(n_space, low, packed, high, i, slice(0, members))
+
+        def aux(i, k):
+            return chosen(n_space, low, packed, high, i, slice(members + k, members + k + 1))
+
+        def adjoint(center, north, south, i):
+            keeping = 1.0 - aux(i, 0) - aux(i, 1) - aux(i, 2) - aux(i, 3)
+            return (
+                center * keeping
+                + aux(i + 1, 0) * south
+                + aux(i - 1, 1) * north
+                + side(aux(i, 2) * center, -1)
+                + side(aux(i, 3) * center, 1)
+            )
+
+        for i in range(1, rows + 3):
+            first_bar[i - 1] = aux(i, 4) * adjoint(bar(i), bar(i - 1), bar(i + 1), i)
+        for r in range(rows):
+            grad[r] = adjoint(first_bar[r + 1], first_bar[r], first_bar[r + 2], r + 2)
+            w2, c2 = second[r], first_ext[r + 1]
+            w1, c1 = first_bar[r + 1], prior(r + 2)
+            sides2 = (first_ext[r], first_ext[r + 2], side(c2, 1), side(c2, -1))
+            sides1 = (prior(r + 1), prior(r + 3), side(c1, 1), side(c1, -1))
+            for k in range(4):
+                term = w2 * (sides2[k] - c2) + w1 * (sides1[k] - c1)
+                coef[0, k * rows + r : k * rows + r + 1] = jnp.sum(term, axis=0, keepdims=True)
+
+    shape = lambda *dims: jax.ShapeDtypeStruct(dims, jnp.float32)
+    return pl.pallas_call(
+        body,
+        out_shape=(shape(rows, members, cols), shape(1, 4 * rows, cols)),
+        in_specs=[VMEM_SPEC] * 7,
+        out_specs=(VMEM_SPEC,) * 2,
+        scratch_shapes=[pltpu.VMEM((rows + 2, members, cols), jnp.float32)],
+        name="backward",
+    )(low_bar, second_bar, high_bar, low, packed, high, first_ext)
 
 
 def local(n_space, n_mem, prior, stencil, sea_mask, sites, data, precision, cotangent):
     members, rows, cols = prior.shape
     total = members * n_mem
-    scale = jnp.sqrt(jnp.float32(total - 1))
-    m = lax.axis_index("mem")
     prior_t = jnp.transpose(prior, (1, 0, 2))
     cot_t = jnp.transpose(cotangent, (1, 0, 2))
+    sea = sea_mask.astype(jnp.float32)[:, None]
     aux = jnp.concatenate(
-        [
-            jnp.transpose(stencil, (1, 0, 2)),
-            sea_mask.astype(jnp.float32)[:, None],
-            jnp.zeros((rows, 3, cols), jnp.float32),
-        ],
-        axis=1,
+        [jnp.transpose(stencil, (1, 0, 2)), sea, jnp.zeros((rows, 3, cols), jnp.float32)], axis=1
     )
     packed = jnp.concatenate([prior_t, aux], axis=1)
     low, high, cot_full = halo_gather(n_space, n_mem, packed[-2:], packed[:2], cot_t, 1)
-    ext = jnp.concatenate([low, packed, high], axis=0)
-    prior_ext = ext[:, :members]
-    coef_ext = jnp.transpose(ext[:, members : members + 4], (1, 0, 2))[:, :, None]
-    sea_ext = ext[:, members + 4][:, None]
-    first_ext = substep(prior_ext, coef_ext[:, 1:-1], sea_ext[1:-1])
-    state = substep(first_ext, coef_ext[:, 2:-2], sea_ext[2:-2])
     cells = jnp.arange(rows * cols, dtype=jnp.int32).reshape(rows, 1, cols)
     onehot = (sites[0][None, :, None] == cells).astype(jnp.float32)
-    picked = dot(state, onehot, (0, 2), (0, 2), HIGHEST)
-    tanh_picked = jnp.tanh(picked)
-    observed = picked + 0.5 * tanh_picked
-    sums = jnp.sum(state, axis=1)
-    sums = jnp.concatenate([sums, jnp.zeros((-rows % 8, cols), jnp.float32)], axis=0)[None]
+    first_ext, state, observed, tanh_picked, sums = forecast(
+        n_space, low, packed, high, onehot, members
+    )
     obs_full, all_sums = gather_members(n_mem, [observed, sums], [0, 0], 3)
-    average = jnp.sum(all_sums, axis=0)[:rows] / total
-    observed_mean = jnp.sum(obs_full, axis=0) / total
-    deviations = (state - average[:, None]) / scale
-    anom_full = (obs_full - observed_mean) * precision / scale
-    obs_anom = (observed - observed_mean) * precision / scale
-    innovation = precision * (data - observed_mean)
-    gram_rows = dot(obs_anom, anom_full, (1,), (1,))
-    cross_rows = dot(deviations, cot_full, (0, 2), (0, 2))
-    pull_rows = jnp.sum(obs_anom * innovation, axis=1)
-    block = jnp.concatenate(
-        [gram_rows, cross_rows, jnp.broadcast_to(pull_rows[:, None], (members, 128))], axis=1
+    block, anom_full, innovation = prepare(
+        n_mem, state, obs_full, all_sums, precision[None], data[None], cot_full
     )
     block = block.reshape(n_space, members // n_space, -1)
-    done = reduce_gather(n_space, n_mem, block, 4)
-    done = done.reshape(total, -1)
+    done = reduce_gather(n_space, n_mem, block, 4).reshape(total, -1)
     second_bar = analyse(
-        done, cot_full, anom_full, innovation[None], precision[None], tanh_picked,
-        onehot, sea_ext[2:-2], members,
+        done, cot_full, anom_full, innovation, precision[None], tanh_picked, onehot, sea, members
     )
     low_bar, high_bar = halo(n_space, second_bar[-2:], second_bar[:2], 5)
-    bar_ext = jnp.concatenate([low_bar, second_bar, high_bar], axis=0)
-    first_bar = sea_ext[1:-1] * transpose_step(bar_ext, coef_ext)
-    coef_part = coef_terms(second_bar, first_ext) + coef_terms(first_bar[1:-1], prior_ext[1:-1])
-    (coef_all,) = gather_members(n_mem, [coef_part.reshape(1, 4 * rows, cols)], [0], 6)
-    prior_grad = transpose_step(first_bar, coef_ext[:, 1:-1])
+    prior_grad, coef_part = backward(
+        n_space, low_bar, second_bar, high_bar, low, packed, high, first_ext
+    )
+    (coef_all,) = gather_members(n_mem, [coef_part], [0], 6)
     coef_total = jnp.sum(coef_all, axis=0).reshape(4, rows, cols)
     return (
         jnp.transpose(prior_grad, (1, 0, 2)),

time: 117 us -> 102 us (0.87)
  other arithmetic: 14.4 us -> 3.57 us
  matrix products: 3.6 us -> 0 us
    pallas_call x0 -> x3, Pallas kernels: none -> 8.42 us  [the longest x1 2.94 us: prepare(): pl.pallas_call(body, out_shape=(shape(members, total + 3 * members), shap...]
    pallas_call x1, Pallas kernels: 40.8 us -> 35.4 us  [reduce_gather(): pl.pallas_call(body, out_shape=jax.ShapeDtypeStruct((n_mem, far, near, he...]
    dot_general x3 -> x0, matrix products: 3.6 us -> none  [dot(): lax.dot_general(a, b, ((a_dims, b_dims), ((), ())), precision=precision,...]
    reduce_sum x5 -> x0, other arithmetic: 3.41 us -> none  [the longest x2 1.46 us: coef_terms(): jnp.sum(weight * (side - center), axis=1)]
    pallas_call x1, Pallas kernels: 11.5 us -> 8.68 us  [halo(): pl.pallas_call(body, out_shape=(shape, shape), in_specs=[VMEM_SPEC] * 2,...]
    concatenate x4 -> x0, other arithmetic: 1.96 us -> none  [the longest x1 1.82 us: local(): jnp.concatenate([gram_rows, cross_rows, jnp.broadcast_to(pull_rows[:, Non...]
    select_n x3 -> x0, other arithmetic: 1.88 us -> none  [masked(): return (jnp.where(s > 0, low, 0.0), jnp.where(s < n_space - 1, high, 0.0))]
    div x2 -> x0, other arithmetic: 1.69 us -> none  [the longest x1 1.68 us: local(): anom_full = (obs_full - observed_mean) * precision / scale]
where the time goes in v3:
time: 102 us; the launch traced here: 101 us
  Pallas kernels  88.8 us (87%)
  local copies, waits for them, and re-layouts  7.77 us (8%)
  other arithmetic  3.57 us (4%)
    pallas_call x1, Pallas kernels, reduce_gather(): pl.pallas_call(body, out_shape=jax.ShapeDtypeStruct((n_mem, far, near, he...  35.4 us
    pallas_call x1, Pallas kernels, halo_gather(): pl.pallas_call(body, out_shape=(shape, shape, jax.ShapeDtypeStruct(tuple(...  14 us
    pallas_call x2, Pallas kernels, gather_members(): pl.pallas_call(body, out_shape=tuple(shapes), in_specs=[VMEM_SPEC] * coun...  11.8 us
    pallas_call x1, Pallas kernels, analyse(): pl.pallas_call(body, out_shape=jax.ShapeDtypeStruct((rows, members, cols)...  10.5 us
    pallas_call x1, Pallas kernels, halo(): pl.pallas_call(body, out_shape=(shape, shape), in_specs=[VMEM_SPEC] * 2,...  8.68 us
    unnamed x8, local copies, waits for them, and re-layouts  5.27 us
    pallas_call x1, Pallas kernels, prepare(): pl.pallas_call(body, out_shape=(shape(members, total + 3 * members), shap...  2.94 us
    pallas_call x1, Pallas kernels, forecast(): pl.pallas_call(body, out_shape=(shape(rows + 2, members, cols), shape(row...  2.76 us

profile of v3, /device:TPU:0, one launch (start us, length us, event | category | flops | bytes accessed | tf_op | source)
XLA Modules:
  0.0 100.9 jit_solution(4010982756223490090)
XLA Ops:
  0.6 0.1 pad.3.clone
  0.7 0.7 convert_element_type.6
  1.4 0.0 copy-start.1
  1.4 0.7 copy.18
  2.1 1.4 %compare_convert_fusion.hot = f32[4,128,128]{2,1,0:T(8,128)} fusion(s32[4,128]{1,0:T(4,128)S(1)} %multiply_add_fusion, s32[128]{0:T(128)} %bitcast.26), kind=kLoop, calls=%fused_computation.3 | loop fusion | flops 131072 | bytes 264704 | tf_op jit(solution)/shard_map/convert_element_type | solution.py:648
  3.5 1.0 copy.17
  4.5 0.1 maximum_maximum_fusion.packed
  4.6 0.0 copy-start
  4.6 1.8 %copy.16 = f32[128,4,128]{2,0,1:T(8,128)} copy(f32[128,4,128]{2,1,0:T(4,128)} %param.13) | data formatting | bytes 524288 | tf_op args[6]
  6.4 0.7 fusion
  7.1 14.0 %halo_gather.1 = (f32[2,136,128]{2,1,0:T(8,128)}, f32[2,136,128]{2,1,0:T(8,128)}, f32[4,512,128]{2,1,0:T(8,128)}) custom-call(f32[2,136,128]{2,1,0:T(8,128)} %get-tuple-element.39.last_ref, f32[2,136,128]{2,1,0:T(8,128)} %get-tuple-element.38.first_ref, f32[4,128,128]{2,1,0:T(8,128)} %bitcast.18), custom_call_target="tpu_custom_call" | custom-call | tf_op jit(solution)/shard_map/halo_gather/pallas_call | solution.py:141
  21.1 0.0 copy-done
  21.1 2.8 %forecast.1 = (f32[6,128,128]{2,1,0:T(8,128)}, f32[4,128,128]{2,1,0:T(8,128)}, f32[128,128]{1,0:T(8,128)}, f32[128,128]{1,0:T(8,128)}, f32[1,8,128]{2,1,0:T(8,128)}) custom-call(f32[2,136,128]{2,1,0:T(8,128)} %get-tuple-element.19.low, f32[4,136,128]{2,1,0:T(8,128)} %copy-done, f32[2,136,128]{2,1,0:T(8,128)} %get-tuple-element.20.high, ...), custom_call_target="tpu_custom_call" | custom-call | tf_op jit(solution)/shard_map/forecast/pallas_call | solution.py:528
  23.9 0.0 copy-done.1
  23.9 6.8 %gather_members.2 = (f32[512,128]{1,0:T(8,128)}, f32[4,8,128]{2,1,0:T(8,128)}) custom-call(f32[128,128]{1,0:T(8,128)} %get-tuple-element.22.refs_0_, f32[1,8,128]{2,1,0:T(8,128)} %get-tuple-element.23.refs_1_), custom_call_target="tpu_custom_call" | custom-call | tf_op jit(solution)/shard_map/gather_members/pallas_call | solution.py:197
  30.7 2.9 %prepare.1 = (f32[128,896]{1,0:T(8,128)}, f32[512,128]{1,0:T(8,128)}, f32[1,128]{1,0:T(1,128)}) custom-call(f32[4,128,128]{2,1,0:T(8,128)} %get-tuple-element.21.state, f32[512,128]{1,0:T(8,128)} %get-tuple-element.24.obs, f32[4,8,128]{2,1,0:T(8,128)} %get-tuple-element.25.sums, f32[1,128]{1,0:T(1,128)} %bitcast.28, f32[1,128]{1,0:T(1,128)} %bitcast.27, ...), custom_call_target="tpu_custom_call" | custom-call | tf_op jit(solution)/shard_map/prepare/pallas_call | solution.py:581
  33.6 35.4 %reduce_gather.1 = f32[4,4,2,16,896]{4,3,2,1,0:T(8,128)} custom-call(f32[8,16,896]{2,1,0:T(8,128)} %bitcast.20), custom_call_target="tpu_custom_call" | custom-call | tf_op jit(solution)/shard_map/reduce_gather/pallas_call | solution.py:342
  69.0 10.5 %analyse.1.second = f32[4,128,128]{2,1,0:T(8,128)} custom-call(f32[512,896]{1,0:T(8,128)} %bitcast.17, f32[4,512,128]{2,1,0:T(8,128)} %get-tuple-element.26.cot, f32[512,128]{1,0:T(8,128)} %get-tuple-element.28.anom, f32[1,128]{1,0:T(1,128)} %get-tuple-element.29.innov, f32[1,128]{1,0:T(1,128)} %bitcast.29, f32[128,128]{1,0:T(8,128)} %get-tuple-element.30.tanh, ...), custom_call_target="tpu_custom_call" | custom-call | flops 1342177280 | bytes 2097152 | tf_op jit(solution)/shard_map/analyse/pallas_call | solution.py:463
  79.6 1.7 %fusion.1 = (f32[2,128,128]{2,1,0:T(8,128)}, f32[2,128,128]{2,1,0:T(8,128)}) fusion(f32[4,128,128]{2,1,0:T(8,128)} %analyse.1.second), kind=kLoop, calls=%fused_computation.8 | loop fusion | bytes 524288 | tf_op jit(solution)/shard_map/slice | solution.py:661
  81.2 8.7 %halo.1 = (f32[2,128,128]{2,1,0:T(8,128)}, f32[2,128,128]{2,1,0:T(8,128)}) custom-call(f32[2,128,128]{2,1,0:T(8,128)} %get-tuple-element.41.last_ref, f32[2,128,128]{2,1,0:T(8,128)} %get-tuple-element.40.first_ref), custom_call_target="tpu_custom_call" | custom-call | tf_op jit(solution)/shard_map/halo/pallas_call | solution.py:84
  89.9 2.7 %backward.1 = (f32[4,128,128]{2,1,0:T(8,128)}, f32[1,16,128]{2,1,0:T(8,128)}) custom-call(f32[2,128,128]{2,1,0:T(8,128)} %get-tuple-element.31.low_bar, f32[4,128,128]{2,1,0:T(8,128)} %analyse.1.second, f32[2,128,128]{2,1,0:T(8,128)} %get-tuple-element.32.high_bar, f32[2,136,128]{2,1,0:T(8,128)} %get-tuple-element.19.low, f32[4,136,128]{2,1,0:T(8,128)} %copy-done, ...), custom_call_target="tpu_custom_call" | custom-call | tf_op jit(solution)/shard_map/backward/pallas_call | solution.py:626
  92.6 1.8 %copy.12 = f32[128,4,128]{2,1,0:T(4,128)} copy(f32[128,4,128]{2,0,1:T(8,128)} %bitcast.21) | data formatting | bytes 524288
  94.5 5.0 %gather_members.3 = f32[4,16,128]{2,1,0:T(8,128)} custom-call(f32[1,16,128]{2,1,0:T(8,128)} %get-tuple-element.35.refs_0_), custom_call_target="tpu_custom_call" | custom-call | tf_op jit(solution)/shard_map/gather_members/pallas_call | solution.py:197
  99.5 0.8 reduce_sum.9
  100.3 0.6 broadcast_multiply_fusion
  (2 shorter events, 0.0 us)
Async XLA Ops:
  1.4 22.5 %copy-start.1 = (f32[4,128]{1,0:T(4,128)}, f32[4,128]{1,0:T(4,128)S(1)}, u32[]{:S(2)}) copy-start(f32[4,128]{1,0:T(4,128)S(1)} %convert_element_type.6) | copy-start | bytes 6148
  4.6 16.5 %copy-start = (f32[4,136,128]{2,1,0:T(8,128)}, f32[4,136,128]{2,1,0:T(8,128)S(1)}, u32[]{:S(2)}) copy-start(f32[4,136,128]{2,1,0:T(8,128)S(1)} %maximum_maximum_fusion.packed) | copy-start | bytes 835588

commit v4 on v3

--- a/solution.py
+++ b/solution.py
@@ -37,6 +37,14 @@
     barrier = pltpu.get_barrier_semaphore()
     has_low, has_high = s > 0, s < n_space - 1
 
+    @pl.when(jnp.logical_not(has_low))
+    def _():
+        low[...] = jnp.zeros_like(low)
+
+    @pl.when(jnp.logical_not(has_high))
+    def _():
+        high[...] = jnp.zeros_like(high)
+
     @pl.when(has_low)
     def _():
         pl.semaphore_signal(barrier, inc=1, device_id=(s - 1, m), device_id_type=MESH)
@@ -74,139 +82,6 @@
             up.wait_send()
 
     return finish
-
-
-def halo(n_space, last, first, ident):
-    def body(last_ref, first_ref, low, high, send, recv):
-        halo_body(n_space, last_ref, first_ref, low, high, send, recv, [])()
-
-    shape = jax.ShapeDtypeStruct(last.shape, last.dtype)
-    low, high = pl.pallas_call(
-        body,
-        out_shape=(shape, shape),
-        in_specs=[VMEM_SPEC] * 2,
-        out_specs=(VMEM_SPEC,) * 2,
-        scratch_shapes=[pltpu.SemaphoreType.DMA((2,)), pltpu.SemaphoreType.DMA((2,))],
-        compiler_params=params(ident),
-        name="halo",
-    )(last, first)
-    return low, high
-
-
-def halo_gather(n_space, n_mem, last, first, block, ident):
-    half = 2 if n_mem % 2 == 0 else 1
-    wide = n_mem // half
-    members = block.shape[1]
-
-    def body(last_ref, first_ref, x, low, high, out, send, recv, own, p_send, p_recv, q_send, q_recv):
-        s, m = lax.axis_index("space"), lax.axis_index("mem")
-        p, q = m // half, lax.rem(m, half)
-        across = [lax.rem(p + k, wide) * half + q for k in range(1, wide)]
-        beside = [p * half + lax.rem(q + k, half) for k in range(1, half)]
-
-        def part(which):
-            return out.at[:, pl.ds(pl.multiple_of(which * members, members), members)]
-
-        mine = pltpu.make_async_copy(x, part(m), own.at[0])
-        mine.start()
-        finish = halo_body(
-            n_space, last_ref, first_ref, low, high, send, recv, [(s, to) for to in across + beside]
-        )
-        copies = []
-        for k, to in enumerate(across):
-            copies.append(remote(x, part(m), p_send.at[k], p_recv.at[k], s, to))
-            copies[-1].start()
-        hops = list(copies)
-        for k, to in enumerate(beside):
-            copies.append(remote(x, part(m), q_send.at[k, 0], q_recv.at[k, 0], s, to))
-            copies[-1].start()
-        for kp, hop in enumerate(hops):
-            from_p = lax.rem(p + wide - kp - 1, wide)
-            hop.wait_recv()
-            piece = part(from_p * half + q)
-            for k, to in enumerate(beside):
-                copies.append(remote(piece, piece, q_send.at[k, kp + 1], q_recv.at[k, kp + 1], s, to))
-                copies[-1].start()
-        finish()
-        mine.wait()
-        for copy in copies[len(hops) :]:
-            copy.wait_recv()
-        for copy in copies:
-            copy.wait_send()
-
-    shape = jax.ShapeDtypeStruct(last.shape, last.dtype)
-    full = list(block.shape)
-    full[1] *= n_mem
-    dma = pltpu.SemaphoreType.DMA
-    low, high, out = pl.pallas_call(
-        body,
-        out_shape=(shape, shape, jax.ShapeDtypeStruct(tuple(full), block.dtype)),
-        in_specs=[VMEM_SPEC] * 3,
-        out_specs=(VMEM_SPEC,) * 3,
-        scratch_shapes=[
-            dma((2,)), dma((2,)), dma((1,)), dma((wide,)), dma((wide,)),
-            dma((half, wide)), dma((half, wide)),
-        ],
-        compiler_params=params(ident),
-        name="halo_gather",
-    )(last, first, block)
-    return low, high, out
-
-
-def gather_members(n_mem, arrays, dims, ident):
-    count = len(arrays)
-
-    def body(*refs):
-        ins, outs = refs[:count], refs[count : 2 * count]
-        send, recv, own = refs[2 * count :]
-        s, m = lax.axis_index("space"), lax.axis_index("mem")
-        barrier = pltpu.get_barrier_semaphore()
-        for k in range(1, n_mem):
-            pl.semaphore_signal(
-                barrier, inc=1, device_id=(s, lax.rem(m + k, n_mem)), device_id_type=MESH
-            )
-
-        def part(i, which):
-            width = arrays[i].shape[dims[i]]
-            where = [slice(None)] * arrays[i].ndim
-            where[dims[i]] = pl.ds(pl.multiple_of(which * width, width), width)
-            return outs[i].at[tuple(where)]
-
-        mine = [pltpu.make_async_copy(ins[i], part(i, m), own.at[i]) for i in range(count)]
-        for copy in mine:
-            copy.start()
-        pl.semaphore_wait(barrier, n_mem - 1)
-        copies = []
-        for k in range(1, n_mem):
-            for i in range(count):
-                copy = remote(
-                    ins[i], part(i, m), send.at[i, k], recv.at[i, k], s, lax.rem(m + k, n_mem)
-                )
-                copy.start()
-                copies.append(copy)
-        for copy in copies:
-            copy.wait()
-        for copy in mine:
-            copy.wait()
-
-    shapes = []
-    for array, dim in zip(arrays, dims):
-        shape = list(array.shape)
-        shape[dim] *= n_mem
-        shapes.append(jax.ShapeDtypeStruct(tuple(shape), array.dtype))
-    return pl.pallas_call(
-        body,
-        out_shape=tuple(shapes),
-        in_specs=[VMEM_SPEC] * count,
-        out_specs=(VMEM_SPEC,) * count,
-        scratch_shapes=[
-            pltpu.SemaphoreType.DMA((count, n_mem)),
-            pltpu.SemaphoreType.DMA((count, n_mem)),
-            pltpu.SemaphoreType.DMA((count,)),
-        ],
-        compiler_params=params(ident),
-        name="gather_members",
-    )(*arrays)
 
 
 def reduce_gather(n_space, n_mem, rows, ident):
@@ -490,11 +365,56 @@
     return jnp.where(s < n_space - 1, high[i - rows - 2, where], 0.0)
 
 
-def forecast(n_space, low, packed, high, onehot, members):
-    rows, _, cols = packed.shape
+def member_sends(n_mem, piece, send, recv):
+    s, m = lax.axis_index("space"), lax.axis_index("mem")
+    copies = []
+    for k in range(1, n_mem):
+        copies.append(remote(piece, piece, send.at[k], recv.at[k], s, lax.rem(m + k, n_mem)))
+        copies[-1].start()
+    return copies
+
+
+def forecast(n_space, n_mem, packed, block, onehot, members, ident):
+    rows, depth, cols = packed.shape
     sites = onehot.shape[1]
-
-    def body(low, packed, high, hot, first, state, observed, tanh, sums):
+    half = 2 if n_mem % 2 == 0 else 1
+    wide = n_mem // half
+
+    def body(
+        packed, x, hot, low, high, out, first, state, observed, tanh, sums,
+        send, recv, own, p_send, p_recv, q_send, q_recv, o_send, o_recv, t_send, t_recv,
+    ):
+        s, m = lax.axis_index("space"), lax.axis_index("mem")
+        p, q = m // half, lax.rem(m, half)
+        across = [lax.rem(p + k, wide) * half + q for k in range(1, wide)]
+        beside = [p * half + lax.rem(q + k, half) for k in range(1, half)]
+
+        def part(which):
+            return out.at[:, pl.ds(pl.multiple_of(which * members, members), members)]
+
+        mine = pltpu.make_async_copy(x, part(m), own.at[0])
+        mine.start()
+        finish = halo_body(
+            n_space, packed.at[pl.ds(rows - 2, 2)], packed.at[pl.ds(0, 2)], low, high, send, recv,
+            [(s, lax.rem(m + k, n_mem)) for k in range(1, n_mem)],
+        )
+        copies = []
+        for k, to in enumerate(across):
+            copies.append(remote(x, part(m), p_send.at[k], p_recv.at[k], s, to))
+            copies[-1].start()
+        hops = list(copies)
+        for k, to in enumerate(beside):
+            copies.append(remote(x, part(m), q_send.at[k, 0], q_recv.at[k, 0], s, to))
+            copies[-1].start()
+        finish()
+        for kp, hop in enumerate(hops):
+            from_p = lax.rem(p + wide - kp - 1, wide)
+            hop.wait_recv()
+            piece = part(from_p * half + q)
+            for k, to in enumerate(beside):
+                copies.append(remote(piece, piece, q_send.at[k, kp + 1], q_recv.at[k, kp + 1], s, to))
+                copies[-1].start()
+
         def row(i):
             return chosen(n_space, low, packed, high, i, slice(0, members))
 
@@ -513,28 +433,47 @@
         for i in range(1, rows + 3):
             first[i - 1] = step(row(i), row(i - 1), row(i + 1), i)
         picked = jnp.zeros((members, sites), jnp.float32)
-        sums[...] = jnp.zeros_like(sums)
+        lines = []
         for r in range(rows):
             state[r] = step(first[r + 1], first[r], first[r + 2], r + 2)
-            sums[0, r : r + 1] = jnp.sum(state[r], axis=0, keepdims=True)
+            lines.append(jnp.sum(state[r], axis=0, keepdims=True))
             picked = picked + lax.dot_general(
                 state[r], hot[r], (((1,), (1,)), ((), ())), precision=HIGHEST,
                 preferred_element_type=jnp.float32,
             )
+        lines.append(jnp.zeros((-rows % 8, cols), jnp.float32))
+        sums[m] = jnp.concatenate(lines, axis=0)
         tanh[...] = jnp.tanh(picked)
-        observed[...] = picked + 0.5 * tanh[...]
+        slot = pl.ds(pl.multiple_of(m * members, members), members)
+        observed[slot, :] = picked + 0.5 * tanh[...]
+        last = member_sends(n_mem, observed.at[slot], o_send, o_recv)
+        last += member_sends(n_mem, sums.at[m], t_send, t_recv)
+        mine.wait()
+        for copy in copies[len(hops) :] + last:
+            copy.wait_recv()
+        for copy in copies + last:
+            copy.wait_send()
 
     shape = lambda *dims: jax.ShapeDtypeStruct(dims, jnp.float32)
+    dma = pltpu.SemaphoreType.DMA
     return pl.pallas_call(
         body,
         out_shape=(
-            shape(rows + 2, members, cols), shape(rows, members, cols), shape(members, sites),
-            shape(members, sites), shape(1, rows + -rows % 8, cols),
+            shape(2, depth, cols), shape(2, depth, cols), shape(rows, n_mem * members, cols),
+            shape(rows + 2, members, cols), shape(rows, members, cols),
+            shape(n_mem * members, sites), shape(members, sites),
+            shape(n_mem, rows + -rows % 8, cols),
         ),
-        in_specs=[VMEM_SPEC] * 4,
-        out_specs=(VMEM_SPEC,) * 5,
+        in_specs=[VMEM_SPEC] * 3,
+        out_specs=(VMEM_SPEC,) * 8,
+        scratch_shapes=[
+            dma((2,)), dma((2,)), dma((1,)), dma((wide,)), dma((wide,)),
+            dma((half, wide)), dma((half, wide)),
+            dma((n_mem,)), dma((n_mem,)), dma((n_mem,)), dma((n_mem,)),
+        ],
+        compiler_params=params(ident),
         name="forecast",
-    )(low, packed, high, onehot)
+    )(packed, block, onehot)
 
 
 def prepare(n_mem, state, obs_full, sums, precision, data, cot_full):
@@ -587,10 +526,19 @@
     )(state, obs_full, sums, precision, data, cot_full)
 
 
-def backward(n_space, low_bar, second_bar, high_bar, low, packed, high, first_ext):
+def backward(n_space, n_mem, second_bar, low, packed, high, first_ext, ident):
     rows, members, cols = second_bar.shape
 
-    def body(low_bar, second, high_bar, low, packed, high, first_ext, grad, coef, first_bar):
+    def body(
+        second, low, packed, high, first_ext, grad, coef, low_bar, high_bar, first_bar,
+        send, recv, c_send, c_recv,
+    ):
+        s, m = lax.axis_index("space"), lax.axis_index("mem")
+        halo_body(
+            n_space, second.at[pl.ds(rows - 2, 2)], second.at[pl.ds(0, 2)], low_bar, high_bar,
+            send, recv, [(s, lax.rem(m + k, n_mem)) for k in range(1, n_mem)],
+        )()
+
         def bar(i):
             return chosen(n_space, low_bar, second, high_bar, i, slice(0, members))
 
@@ -612,25 +560,37 @@
 
         for i in range(1, rows + 3):
             first_bar[i - 1] = aux(i, 4) * adjoint(bar(i), bar(i - 1), bar(i + 1), i)
+        lines = [[None] * rows for _ in range(4)]
         for r in range(rows):
-            grad[r] = adjoint(first_bar[r + 1], first_bar[r], first_bar[r + 2], r + 2)
             w2, c2 = second[r], first_ext[r + 1]
             w1, c1 = first_bar[r + 1], prior(r + 2)
             sides2 = (first_ext[r], first_ext[r + 2], side(c2, 1), side(c2, -1))
             sides1 = (prior(r + 1), prior(r + 3), side(c1, 1), side(c1, -1))
             for k in range(4):
                 term = w2 * (sides2[k] - c2) + w1 * (sides1[k] - c1)
-                coef[0, k * rows + r : k * rows + r + 1] = jnp.sum(term, axis=0, keepdims=True)
+                lines[k][r] = jnp.sum(term, axis=0, keepdims=True)
+        coef[m] = jnp.concatenate([line for group in lines for line in group], axis=0)
+        copies = member_sends(n_mem, coef.at[m], c_send, c_recv)
+        for r in range(rows):
+            grad[r] = adjoint(first_bar[r + 1], first_bar[r], first_bar[r + 2], r + 2)
+        for copy in copies:
+            copy.wait()
 
     shape = lambda *dims: jax.ShapeDtypeStruct(dims, jnp.float32)
+    edge = pltpu.VMEM((2, members, cols), jnp.float32)
+    dma = pltpu.SemaphoreType.DMA
     return pl.pallas_call(
         body,
-        out_shape=(shape(rows, members, cols), shape(1, 4 * rows, cols)),
-        in_specs=[VMEM_SPEC] * 7,
+        out_shape=(shape(rows, members, cols), shape(n_mem, 4 * rows, cols)),
+        in_specs=[VMEM_SPEC] * 5,
         out_specs=(VMEM_SPEC,) * 2,
-        scratch_shapes=[pltpu.VMEM((rows + 2, members, cols), jnp.float32)],
+        scratch_shapes=[
+            edge, edge, pltpu.VMEM((rows + 2, members, cols), jnp.float32),
+            dma((2,)), dma((2,)), dma((n_mem,)), dma((n_mem,)),
+        ],
+        compiler_params=params(ident),
         name="backward",
-    )(low_bar, second_bar, high_bar, low, packed, high, first_ext)
+    )(second_bar, low, packed, high, first_ext)
 
 
 def local(n_space, n_mem, prior, stencil, sea_mask, sites, data, precision, cotangent):
@@ -643,26 +603,22 @@
         [jnp.transpose(stencil, (1, 0, 2)), sea, jnp.zeros((rows, 3, cols), jnp.float32)], axis=1
     )
     packed = jnp.concatenate([prior_t, aux], axis=1)
-    low, high, cot_full = halo_gather(n_space, n_mem, packed[-2:], packed[:2], cot_t, 1)
     cells = jnp.arange(rows * cols, dtype=jnp.int32).reshape(rows, 1, cols)
     onehot = (sites[0][None, :, None] == cells).astype(jnp.float32)
-    first_ext, state, observed, tanh_picked, sums = forecast(
-        n_space, low, packed, high, onehot, members
-    )
-    obs_full, all_sums = gather_members(n_mem, [observed, sums], [0, 0], 3)
+    low, high, cot_full, first_ext, state, obs_full, tanh_picked, all_sums = forecast(
+        n_space, n_mem, packed, cot_t, onehot, members, 1
+    )
     block, anom_full, innovation = prepare(
         n_mem, state, obs_full, all_sums, precision[None], data[None], cot_full
     )
     block = block.reshape(n_space, members // n_space, -1)
-    done = reduce_gather(n_space, n_mem, block, 4).reshape(total, -1)
+    done = reduce_gather(n_space, n_mem, block, 3).reshape(total, -1)
     second_bar = analyse(
         done, cot_full, anom_full, innovation, precision[None], tanh_picked, onehot, sea, members
     )
-    low_bar, high_bar = halo(n_space, second_bar[-2:], second_bar[:2], 5)
-    prior_grad, coef_part = backward(
-        n_space, low_bar, second_bar, high_bar, low, packed, high, first_ext
-    )
-    (coef_all,) = gather_members(n_mem, [coef_part], [0], 6)
+    prior_grad, coef_all = backward(
+        n_space, n_mem, second_bar, low, packed, high, first_ext, 2
+    )
     coef_total = jnp.sum(coef_all, axis=0).reshape(4, rows, cols)
     return (
         jnp.transpose(prior_grad, (1, 0, 2)),

time: 102 us -> 90.7 us (0.89)
  Pallas kernels: 88.8 us -> 80 us
  local copies, waits for them, and re-layouts: 7.77 us -> 5.24 us
    pallas_call x6 -> x2, Pallas kernels: 39.9 us -> 32.6 us  [the longest x1 18.7 us: forecast(): pl.pallas_call(body, out_shape=(shape(2, depth, cols), shape(2, depth, co...]
    slice x2 -> x0, local copies, waits for them, and re-layouts: 2.43 us -> none  [the longest x1 1.68 us: local(): low_bar, high_bar = halo(n_space, second_bar[-2:], second_bar[:2], 5)]
    pallas_call x1, Pallas kernels: 35.4 us -> 34 us  [reduce_gather(): pl.pallas_call(body, out_shape=jax.ShapeDtypeStruct((n_mem, far, near, he...]
    unnamed x8 -> x6, local copies, waits for them, and re-layouts: 5.27 us -> 5.16 us
where the time goes in v4:
time: 90.7 us; the launch traced here: 90.2 us
  Pallas kernels  80 us (88%)
  local copies, waits for them, and re-layouts  5.24 us (6%)
  other arithmetic  4.28 us (5%)
    pallas_call x1, Pallas kernels, reduce_gather(): pl.pallas_call(body, out_shape=jax.ShapeDtypeStruct((n_mem, far, near, he...  34 us
    pallas_call x1, Pallas kernels, forecast(): pl.pallas_call(body, out_shape=(shape(2, depth, cols), shape(2, depth, co...  18.7 us
    pallas_call x1, Pallas kernels, backward(): pl.pallas_call(body, out_shape=(shape(rows, members, cols), shape(n_mem,...  13.9 us
    pallas_call x1, Pallas kernels, analyse(): pl.pallas_call(body, out_shape=jax.ShapeDtypeStruct((rows, members, cols)...  10.6 us
    unnamed x6, local copies, waits for them, and re-layouts  5.16 us
    pallas_call x1, Pallas kernels, prepare(): pl.pallas_call(body, out_shape=(shape(members, total + 3 * members), shap...  2.95 us

profile of v4, /device:TPU:0, one launch (start us, length us, event | category | flops | bytes accessed | tf_op | source)
XLA Modules:
  0.0 90.2 jit_solution(2866665007250173637)
XLA Ops:
  0.6 0.1 pad.3.clone
  0.7 0.7 convert_element_type.6
  1.4 0.0 copy-start
  1.4 0.7 copy.18
  2.1 1.4 %compare_convert_fusion.hot = f32[4,128,128]{2,1,0:T(8,128)} fusion(s32[4,128]{1,0:T(4,128)S(1)} %multiply_add_fusion, s32[128]{0:T(128)} %bitcast.26), kind=kLoop, calls=%fused_computation.3 | loop fusion | flops 131072 | bytes 264704 | tf_op jit(solution)/shard_map/convert_element_type | solution.py:607
  3.5 1.0 %copy.17 = f32[128,4,128]{2,0,1:T(8,128)S(1)} copy(f32[128,4,128]{2,1,0:T(4,128)} %param.7) | data formatting | bytes 524288 | tf_op args[0]
  4.5 0.8 maximum_maximum_fusion.packed
  5.3 1.7 %copy.16 = f32[128,4,128]{2,0,1:T(8,128)} copy(f32[128,4,128]{2,1,0:T(4,128)} %param.13) | data formatting | bytes 524288 | tf_op args[6]
  7.0 18.7 %forecast.1 = (f32[2,136,128]{2,1,0:T(8,128)}, f32[2,136,128]{2,1,0:T(8,128)}, f32[4,512,128]{2,1,0:T(8,128)}, f32[6,128,128]{2,1,0:T(8,128)}, f32[4,128,128]{2,...) custom-call(f32[4,136,128]{2,1,0:T(8,128)} %maximum_maximum_fusion.packed, ...), custom_call_target="tpu_custom_call" | custom-call | tf_op jit(solution)/shard_map/forecast/pallas_call | solution.py:459
  25.7 2.9 %prepare.1 = (f32[128,896]{1,0:T(8,128)}, f32[512,128]{1,0:T(8,128)}, f32[1,128]{1,0:T(1,128)}) custom-call(f32[4,128,128]{2,1,0:T(8,128)} %get-tuple-element.15.state, f32[512,128]{1,0:T(8,128)} %get-tuple-element.16.obs, f32[4,8,128]{2,1,0:T(8,128)} %get-tuple-element.17.sums, f32[1,128]{1,0:T(1,128)} %bitcast.28, f32[1,128]{1,0:T(1,128)} %bitcast.27, ...), custom_call_target="tpu_custom_call" | custom-call | tf_op jit(solution)/shard_map/prepare/pallas_call | solution.py:520
  28.6 0.0 copy-done
  28.6 34.0 %reduce_gather.1 = f32[4,4,2,16,896]{4,3,2,1,0:T(8,128)} custom-call(f32[8,16,896]{2,1,0:T(8,128)} %bitcast.20), custom_call_target="tpu_custom_call" | custom-call | tf_op jit(solution)/shard_map/reduce_gather/pallas_call | solution.py:217
  62.6 10.6 %analyse.1.second = f32[4,128,128]{2,1,0:T(8,128)} custom-call(f32[512,896]{1,0:T(8,128)} %bitcast.17, f32[4,512,128]{2,1,0:T(8,128)} %get-tuple-element.18.cot, f32[512,128]{1,0:T(8,128)} %get-tuple-element.20.anom, f32[1,128]{1,0:T(1,128)} %get-tuple-element.21.innov, f32[1,128]{1,0:T(1,128)} %bitcast.29, f32[128,128]{1,0:T(8,128)} %get-tuple-element.22.tanh, ...), custom_call_target="tpu_custom_call" | custom-call | flops 1342177280 | bytes 2097152 | tf_op jit(solution)/shard_map/analyse/pallas_call | solution.py:338
  73.2 13.9 %backward.1 = (f32[4,128,128]{2,1,0:T(8,128)}, f32[4,16,128]{2,1,0:T(8,128)}) custom-call(f32[4,128,128]{2,1,0:T(8,128)} %analyse.1.second, f32[2,136,128]{2,1,0:T(8,128)} %get-tuple-element.23.low, f32[4,136,128]{2,1,0:T(8,128)} %maximum_maximum_fusion.packed, f32[2,136,128]{2,1,0:T(8,128)} %get-tuple-element.24.high, ...), custom_call_target="tpu_custom_call" | custom-call | tf_op jit(solution)/shard_map/backward/pallas_call | solution.py:582
  87.0 1.8 %copy.12 = f32[128,4,128]{2,1,0:T(4,128)} copy(f32[128,4,128]{2,0,1:T(8,128)} %bitcast.21) | data formatting | bytes 524288
  88.9 0.8 reduce_sum.9
  89.6 0.6 broadcast_multiply_fusion
  (2 shorter events, 0.0 us)
Async XLA Ops:
  1.4 27.2 %copy-start = (f32[4,128]{1,0:T(4,128)}, f32[4,128]{1,0:T(4,128)S(1)}, u32[]{:S(2)}) copy-start(f32[4,128]{1,0:T(4,128)S(1)} %convert_element_type.6) | copy-start | bytes 6148
